TPU v7x, 32 devices: a whole 2x2x4 slice. The times are simulated.
32 devices in a mesh: rows: 2 (over x), cent: 16 (over z, y, core).
Axes of the slice: x: 2, y: 2, z: 4, core: 2. Of those that a mesh axis runs over, the one named last changes fastest.
Arguments:
- embeddings: bfloat16 [2048, 768], P(('rows', 'cent')), may hold values from -33 to 33
- centroids: bfloat16 [2048, 768], P('cent'), may hold values from -4 to 4
- group_length: int32 [2], P('rows'), may hold values from 256 to 1024, as said below
Outputs:
- new_centroids: bfloat16 [2048, 768], P('cent')
- new_moments: bfloat16 [2048, 768], P('cent')
- loglik: float32 [2048], P(('rows', 'cent'))
Inputs may be any that keep to these rules, and one draw needn't show every extreme that they name: Row group g uses its first group_length[g] of its 1024 row slots; at least one group uses all of them.
All inputs are finite; a program needn't handle non-finite values.
Results may differ from a plain program's by a relative error of at most 0.0047.
Values may be sent and summed in bfloat16 or wider, within the bound.
A program may use at most 64 MiB of HBM per device.

v0:
```python
import functools
import math

import jax
import jax.numpy as jnp
from jax import lax
from jax.experimental import pallas as pl
from jax.experimental.pallas import tpu as pltpu
from jax.sharding import PartitionSpec as P

score_factor = 3.0
prior_weight = 1.0
MESH = pl.DeviceIdType.MESH
contract_width = (((1,), (1,)), ((), ()))
contract_rows = (((1,), (0,)), ((), ()))


def kernel(
    groups, shards, column_step, split,
    length_ref, emb_hbm, cent_hbm,
    cent_out, mom_out, lik_out, inverse_out,
    cent_ref, rows_all, squares, weights, parts, stats, masses,
    own_sem, cent_sem, z_send, z_recv, y_send, y_recv, c_send, c_recv,
    p_send, p_recv, s_send, s_recv, m_send, m_recv,
):
    g = lax.axis_index("rows")
    i = lax.axis_index("cent")
    row_count, width = emb_hbm.shape
    cents = cent_ref.shape[0]
    total = shards * row_count
    piece_rows = row_count // split
    line = shards // 4
    spot = lax.rem(i, 4)
    place = i // 4
    core = lax.rem(i, 2)
    core_peer = i + 1 - 2 * core
    y_spot = lax.rem(spot + 2, 4)
    y_peer = place * 4 + y_spot
    factor = score_factor / math.sqrt(width)

    def across(step):
        return lax.rem(g + step, groups)

    def signal(peer):
        pl.semaphore_signal(barrier, inc=1, device_id=peer, device_id_type=MESH)

    barrier = pltpu.get_barrier_semaphore()
    for peer in [(g, y_peer), (g, core_peer)] + [(across(s), i) for s in range(1, groups)]:
        signal(peer)
    has_right = place < line - 1
    has_left = place > 0
    pl.when(has_right)(lambda: signal((g, i + 4)))
    pl.when(has_left)(lambda: signal((g, i - 4)))
    own = [
        pltpu.make_async_copy(
            emb_hbm.at[pl.ds(h * piece_rows, piece_rows)], rows_all.at[i * split + h], own_sem.at[h]
        )
        for h in range(split)
    ]
    for copy in own:
        copy.start()
    cent_copy = pltpu.make_async_copy(cent_hbm, cent_ref, cent_sem)
    cent_copy.start()
    for copy in own:
        copy.wait()
    sides = has_right.astype(jnp.int32) + has_left.astype(jnp.int32)
    pl.semaphore_wait(barrier, 1 + groups + sides)

    def describe(src, dst, send_sem, recv_sem, peer):
        return pltpu.make_async_remote_copy(
            src_ref=src, dst_ref=dst, send_sem=send_sem, recv_sem=recv_sem,
            device_id=peer, device_id_type=MESH,
        )

    def send(*spec):
        copy = describe(*spec)
        copy.start()
        return copy

    def z_copy(unit, way, s, h):
        slot = rows_all.at[unit]
        peer = (g, i + 4 if way == 0 else i - 4)
        return describe(slot, slot, z_send.at[way, s, h], z_recv.at[way, s, h], peer)

    def y_copy(unit, k, h):
        slot = rows_all.at[unit]
        return describe(slot, slot, y_send.at[k, h], y_recv.at[k, h], (g, y_peer))

    def c_copy(unit, k, h):
        slot = rows_all.at[unit]
        return describe(slot, slot, c_send.at[k, h], c_recv.at[k, h], (g, core_peer))

    def square(unit):
        wide = rows_all[unit].astype(jnp.float32)
        squares[unit] = (wide * wide).astype(jnp.bfloat16)

    steps = 2 * line - 1
    order = [(way, s) for s in range(1, line) for way in range(2)]

    def present(way, s):
        return place >= s if way == 0 else place + s < line

    def unit_of(way, s, where, h):
        source = place - s if way == 0 else place + s
        return (source * 4 + where) * split + h

    for h in range(split):
        unit = i * split + h
        pl.when(has_right)(lambda: z_copy(unit, 0, 1, h).start())
        pl.when(has_left)(lambda: z_copy(unit, 1, 1, h).start())
        y_copy(unit, 0, h).start()
        c_copy(unit, 0, h).start()
    for h in range(split):
        square(i * split + h)
    for k, (way, s) in enumerate(order, 1):
        for h in range(split):
            def relay():
                unit = unit_of(way, s, spot, h)
                z_copy(unit, way, s, h).wait_recv()
                onward = has_right if way == 0 else has_left
                if s + 1 < line:
                    pl.when(onward)(lambda: z_copy(unit, way, s + 1, h).start())
                y_copy(unit, k, h).start()
                c_copy(unit, k, h).start()
                square(unit)

            pl.when(present(way, s))(relay)
    for h in range(split):
        unit = unit_of(0, 0, y_spot, h)
        y_copy(unit, 0, h).wait_recv()
        c_copy(unit, steps, h).start()
        square(unit)
    for k, (way, s) in enumerate(order, 1):
        for h in range(split):
            def pass_on():
                unit = unit_of(way, s, y_spot, h)
                y_copy(unit, k, h).wait_recv()
                c_copy(unit, steps + k, h).start()
                square(unit)

            pl.when(present(way, s))(pass_on)
    other = spot + 1 - 2 * core
    for j, where in enumerate((other, lax.rem(other + 2, 4))):
        for h in range(split):
            unit = unit_of(0, 0, where, h)
            c_copy(unit, j * steps, h).wait_recv()
            square(unit)
        for k, (way, s) in enumerate(order, 1):
            for h in range(split):
                def take():
                    unit = unit_of(way, s, where, h)
                    c_copy(unit, j * steps + k, h).wait_recv()
                    square(unit)

                pl.when(present(way, s))(take)
    sent = []
    cent_copy.wait()
    cent_wide = cent_ref[...].astype(jnp.float32)
    half_norm = 0.5 * jnp.sum(cent_wide * cent_wide, axis=1, keepdims=True)

    slots = split * max(1, min(shards, 512 // row_count))
    chunk = slots * piece_rows
    chunks = shards * split // slots

    def score(k, carry):
        first = k * slots
        columns = k * chunk
        if not isinstance(k, int):
            columns = pl.multiple_of(columns, chunk)
        block = rows_all[pl.ds(first, slots)].reshape(chunk, width)
        inner = lax.dot_general(
            cent_ref[...], block, contract_width, preferred_element_type=jnp.float32
        )
        logits = factor * (inner - half_norm)
        peak = jnp.max(logits, axis=0, keepdims=True)
        weight = jnp.exp(logits - peak)
        weights[:, pl.ds(columns, chunk)] = weight
        parts[0, 0:1, pl.ds(columns, chunk)] = peak
        parts[0, 1:2, pl.ds(columns, chunk)] = jnp.sum(weight, axis=0, keepdims=True)
        return carry

    for k in range(chunks) if chunks <= 4 else ():
        score(k, 0)
    if chunks > 4:
        lax.fori_loop(0, chunks, score, 0)

    own_peak = parts[0, 0:1, :]

    def joined(part_list):
        highest = part_list[0][0]
        for peak, _ in part_list[1:]:
            highest = jnp.maximum(highest, peak)
        amount = None
        for peak, exp_sum in part_list:
            term = exp_sum * jnp.exp(peak - highest)
            amount = term if amount is None else amount + term
        return highest, amount

    def part(k):
        return parts[k, 0:1, :], parts[k, 1:2, :]

    hop = send(parts.at[0], parts.at[1], p_send.at[0], p_recv.at[0], (g, core_peer))

    hop.wait()
    peak, amount = joined([part(0), part(1)])
    parts[2, 0:1, :] = peak
    parts[2, 1:2, :] = amount
    hops = []
    for k in range(2 * line - 1, 0, -1):
        peer = lax.rem(place + k // 2, line) * 4 + lax.rem(spot + 2 * (k % 2), 4)
        hops.append(send(parts.at[2], parts.at[2 + k], p_send.at[k], p_recv.at[k], (g, peer)))
    for hop in hops:
        hop.wait_recv()
    sent += hops
    peak, amount = joined([part(2 + k) for k in range(2 * line)])
    lse = peak + jnp.log(amount)
    valid = lax.broadcasted_iota(jnp.int32, (1, total), 1) < length_ref[0]
    scale = jnp.where(valid, jnp.exp(own_peak - lse), 0.0)
    resp = (weights[...] * scale).astype(jnp.bfloat16)

    ones = jnp.ones((8, total), jnp.bfloat16)
    masses[g] = lax.dot_general(ones, resp, contract_width, preferred_element_type=jnp.float32)
    s_copies = {}
    for s in range(1, groups):
        sent.append(
            send(masses.at[g], masses.at[g], m_send.at[s], m_recv.at[s], (across(s), i))
        )
    m_copies = sent[len(sent) - (groups - 1):]
    pieces = 2 * (width // column_step)
    for k in range(pieces):
        left = (k // 2) * column_step
        source = rows_all if k % 2 == 0 else squares
        block = source[:, :, left:left + column_step].reshape(total, column_step)
        sums = lax.dot_general(resp, block, contract_rows, preferred_element_type=jnp.float32)
        stats[g, k] = sums.astype(jnp.bfloat16)
        for s in range(1, groups):
            s_copies[k, s] = send(
                stats.at[g, k], stats.at[g, k], s_send.at[k, s], s_recv.at[k, s], (across(s), i)
            )

    own_lik = jnp.where(valid, lse, 0.0)
    pick = own_lik[:, 0:row_count]
    for j in range(1, shards):
        pick = jnp.where(i == j, own_lik[:, j * row_count:(j + 1) * row_count], pick)
    lik_out[...] = pick

    for copy in m_copies:
        copy.wait_recv()
    mass = masses[0, 0:1, :]
    for r in range(1, groups):
        mass = mass + masses[r, 0:1, :]
    inverse = 1.0 / (mass + prior_weight)
    inverse_out[...] = jnp.transpose(jnp.broadcast_to(inverse, (cents, cents)))
    for k in range(pieces):
        for s in range(1, groups):
            s_copies[k, s].wait_recv()
        left = (k // 2) * column_step
        sums = stats[0, k].astype(jnp.float32)
        for r in range(1, groups):
            sums = sums + stats[r, k].astype(jnp.float32)
        if k % 2 == 0:
            sums = sums + prior_weight * cent_ref[:, left:left + column_step].astype(jnp.float32)
            cent_out[:, left:left + column_step] = sums
        else:
            mom_out[:, left:left + column_step] = sums + prior_weight
    for h in range(split):
        unit = i * split + h
        pl.when(has_right)(lambda: z_copy(unit, 0, 1, h).wait_send())
        pl.when(has_left)(lambda: z_copy(unit, 1, 1, h).wait_send())
        y_copy(unit, 0, h).wait_send()
        c_copy(unit, 0, h).wait_send()
        c_copy(unit_of(0, 0, y_spot, h), steps, h).wait_send()
    for k, (way, s) in enumerate(order, 1):
        for h in range(split):
            def finish():
                unit = unit_of(way, s, spot, h)
                onward = has_right if way == 0 else has_left
                if s + 1 < line:
                    pl.when(onward)(lambda: z_copy(unit, way, s + 1, h).wait_send())
                y_copy(unit, k, h).wait_send()
                c_copy(unit, k, h).wait_send()
                c_copy(unit_of(way, s, y_spot, h), steps + k, h).wait_send()

            pl.when(present(way, s))(finish)
    for copy in sent + list(s_copies.values()):
        copy.wait_send()


def solution(mesh):
    groups = mesh.shape["rows"]
    shards = mesh.shape["cent"]
    line = shards // 4

    def step(embeddings, centroids, group_length):
        row_count, width = embeddings.shape
        cents = centroids.shape[0]
        total = row_count * shards
        column_step = 256 if width % 256 == 0 else width
        pieces = 2 * (width // column_step)
        split = 2 if row_count % 32 == 0 else 1
        vmem = pl.BlockSpec(memory_space=pltpu.VMEM)
        hbm = pl.BlockSpec(memory_space=pltpu.HBM)
        held = 4 * total * width + 4 * cents * total + 2 * (groups * 2 + 1) * cents * width
        steps = 2 * line - 1
        dma = pltpu.SemaphoreType.DMA
        cent_sums, moment_sums, loglik, inverse = pl.pallas_call(
            functools.partial(kernel, groups, shards, column_step, split),
            out_shape=(
                jax.ShapeDtypeStruct((cents, width), jnp.float32),
                jax.ShapeDtypeStruct((cents, width), jnp.float32),
                jax.ShapeDtypeStruct((1, row_count), jnp.float32),
                jax.ShapeDtypeStruct((cents, cents), jnp.float32),
            ),
            in_specs=[pl.BlockSpec(memory_space=pltpu.SMEM), hbm, hbm],
            out_specs=(vmem, vmem, vmem, vmem),
            scratch_shapes=[
                pltpu.VMEM((cents, width), jnp.bfloat16),
                pltpu.VMEM((shards * split, row_count // split, width), jnp.bfloat16),
                pltpu.VMEM((shards * split, row_count // split, width), jnp.bfloat16),
                pltpu.VMEM((cents, total), jnp.float32),
                pltpu.VMEM((2 + 2 * line, 2, total), jnp.float32),
                pltpu.VMEM((groups, pieces, cents, column_step), jnp.bfloat16),
                pltpu.VMEM((groups, 8, cents), jnp.float32),
                dma((split,)), dma, dma((2, line, split)), dma((2, line, split)),
                dma((steps, split)), dma((steps, split)),
                dma((2 * steps, split)), dma((2 * steps, split)),
                dma((2 * line,)), dma((2 * line,)),
                dma((pieces, groups)), dma((pieces, groups)),
                dma((groups,)), dma((groups,)),
            ],
            compiler_params=pltpu.CompilerParams(
                collective_id=0, has_side_effects=True, vmem_limit_bytes=2 * held + 4 * 1024 * 1024
            ),
            name="soft_em",
        )(group_length, pltpu.with_memory_space_constraint(embeddings, pltpu.HBM), pltpu.with_memory_space_constraint(centroids, pltpu.HBM))
        new_centroids = (cent_sums * inverse[:, 0:1]).astype(jnp.bfloat16)
        new_moments = (moment_sums * inverse[:, 0:1]).astype(jnp.bfloat16)
        return new_centroids, new_moments, loglik.reshape(row_count)

    return jax.shard_map(
        step,
        mesh=mesh,
        in_specs=(P(("rows", "cent"), None), P("cent", None), P("rows")),
        out_specs=(P("cent", None), P("cent", None), P(("rows", "cent"))),
        check_vma=False,
    )
```

profile of v0, /device:TPU:0, one launch (start us, length us, event | category | flops | bytes accessed | tf_op | source)
XLA Modules:
  0.0 38.4 jit_solution(15215355789312995771)
XLA Ops:
  1.3 35.7 %soft_em.1 = (f32[128,768]{1,0:T(8,128)S(1)}, f32[128,768]{1,0:T(8,128)S(1)}, f32[1,64]{1,0:T(1,128)S(1)}, f32[128,128]{1,0:T(8,128)S(1)}) custom-call(s32[1]{0:T(128)S(6)} %copy.7.length_ref, bf16[64,768]{1,0:T(8,128)(2,1)} %emb_hbm.1, bf16[128,768]{1,0:T(8,128)(2,1)} %cent_hbm.1), custom_call_target="tpu_custom_call" | custom-call | tf_op jit(solution)/shard_map/soft_em/pallas_call | solution.py:306
  36.9 0.1 slice_reduce_fusion
  37.0 0.9 %multiply_convert_fusion = (bf16[128,768]{1,0:T(8,128)(2,1)}, bf16[128,768]{1,0:T(8,128)(2,1)}) fusion(f32[128,768]{1,0:T(8,128)S(1)} %get-tuple-element.9, f32[128]{0:T(128)S(1)} %slice_reduce_fusion, f32[128,768]{1,0:T(8,128)S(1)} %get-tuple-element.7), kind=kLoop, calls=%fused_computation | loop fusion | flops 393216 | bytes 1180160 | tf_op jit(solution)/shard_map/convert_element_type | solution.py:337
  37.9 0.5 %copy.8 = f32[64]{0:T(128)} copy(f32[64]{0:T(128)S(1)} %bitcast.1) | data formatting | bytes 512
where the time goes:
time: 38.6 us; the launch traced here: 38.4 us
  Pallas kernels  35.7 us (92%)
  between operations  1.29 us (3%)
  other arithmetic  0.87 us (2%)
  local copies, waits for them, and re-layouts  0.61 us (2%)
    pallas_call x1, Pallas kernels, step(): pl.pallas_call(functools.partial(kernel, groups, shards, column_step, spl...  35.7 us
    convert_element_type x1, other arithmetic, step(): new_moments = (moment_sums * inverse[:, 0:1]).astype(jnp.bfloat16)  0.87 us

commit v1 on v0

--- a/solution.py
+++ b/solution.py
@@ -15,7 +15,10 @@
 contract_rows = (((1,), (0,)), ((), ()))
 
 
-def kernel(
+lanes = 128
+
+
+def sums_kernel(
     groups, shards, column_step, split,
     length_ref, emb_hbm, cent_hbm,
     cent_out, mom_out, lik_out, inverse_out,
@@ -286,6 +289,388 @@
         copy.wait_send()
 
 
+def gather_kernel(
+    shards, split,
+    length_ref, emb_hbm, cent_hbm,
+    cent_out, mom_out, lik_out, inverse_out,
+    cent_ref, rows_all, weights, resp, peaks, pair, parts, lses,
+    own_sem, cent_sem, ready, o_send, z_send, z_recv, y_send, y_recv, x_send, x_recv,
+    c_send, c_recv, q_send, q_recv, p_send, p_recv, l_send, l_recv,
+):
+    g = lax.axis_index("rows")
+    i = lax.axis_index("cent")
+    row_count, width = emb_hbm.shape
+    cents = cent_ref.shape[0]
+    total = shards * row_count
+    piece = row_count // split
+    line = shards // 4
+    chunk = 4 * row_count
+    spread = chunk // lanes
+    spot = lax.rem(i, 4)
+    place = i // 4
+    core = lax.rem(i, 2)
+    core_peer = i + 1 - 2 * core
+    core_spot = spot + 1 - 2 * core
+    y_spot = lax.rem(spot + 2, 4)
+    core_y_spot = lax.rem(core_spot + 2, 4)
+    y_peer = place * 4 + y_spot
+    there = 1 - g
+    factor = score_factor / math.sqrt(width)
+
+    def signal(sem, peer):
+        pl.semaphore_signal(sem, inc=1, device_id=peer, device_id_type=MESH)
+
+    barrier = pltpu.get_barrier_semaphore()
+    has_right = place < line - 1
+    has_left = place > 0
+    pl.when(has_right)(lambda: signal(barrier, (g, i + 4)))
+    pl.when(has_left)(lambda: signal(barrier, (g, i - 4)))
+    for peer in [(g, y_peer), (there, i), (g, core_peer)]:
+        signal(barrier, peer)
+    own = [
+        pltpu.make_async_copy(
+            emb_hbm.at[pl.ds(h * piece, piece)],
+            rows_all.at[g, i, pl.ds(h * piece, piece)], own_sem.at[h],
+        )
+        for h in range(split)
+    ]
+    for copy in own:
+        copy.start()
+    cent_copy = pltpu.make_async_copy(cent_hbm, cent_ref, cent_sem)
+    cent_copy.start()
+    for copy in own:
+        copy.wait()
+    sides = has_right.astype(jnp.int32) + has_left.astype(jnp.int32)
+    pl.semaphore_wait(barrier, 3 + sides)
+
+    def slot(group, q, where, h):
+        return rows_all.at[group, q * 4 + where, pl.ds(h * piece, piece)]
+
+    def move(ref, send_sem, recv_sem, peer):
+        return pltpu.make_async_remote_copy(
+            src_ref=ref, dst_ref=ref, send_sem=send_sem, recv_sem=recv_sem,
+            device_id=peer, device_id_type=MESH,
+        )
+
+    def z_own(way, s, h):
+        peer = (g, i + 4 * s if way == 0 else i - 4 * s)
+        return move(slot(g, place, spot, h), o_send.at[way, s, h], z_recv.at[place, h], peer)
+
+    def z_move(way, q, h):
+        peer = (g, i + 4 if way == 0 else i - 4)
+        return move(slot(g, q, spot, h), z_send.at[q, h], z_recv.at[q, h], peer)
+
+    def y_move(q, h):
+        return move(slot(g, q, spot, h), y_send.at[q, h], y_recv.at[q, h], (g, y_peer))
+
+    def y_come(q, h):
+        return move(slot(g, q, y_spot, h), y_send.at[q, h], y_recv.at[q, h], (g, y_peer))
+
+    def x_move(q, side, h):
+        where = spot if side == 0 else y_spot
+        return move(slot(g, q, where, h), x_send.at[q, side, h], x_recv.at[q, side, h], (there, i))
+
+    def x_come(q, side, h):
+        where = spot if side == 0 else y_spot
+        return move(
+            slot(there, q, where, h), x_send.at[q, side, h], x_recv.at[q, side, h], (there, i)
+        )
+
+    def c_move(mine, q, side, h):
+        where = spot if side == 0 else y_spot
+        t = 0 if mine else 1
+        return move(
+            slot(g if mine else there, q, where, h),
+            c_send.at[t, q, side, h], c_recv.at[t, q, side, h], (g, core_peer),
+        )
+
+    def c_come(mine, q, side, h):
+        where = core_spot if side == 0 else core_y_spot
+        t = 0 if mine else 1
+        return move(
+            slot(g if mine else there, q, where, h),
+            c_send.at[t, q, side, h], c_recv.at[t, q, side, h], (g, core_peer),
+        )
+
+    def source(way, s):
+        return place - s if way == 0 else place + s
+
+    def present(way, s):
+        return place >= s if way == 0 else place + s < line
+
+    def onward(way, s):
+        if way == 0:
+            return jnp.logical_and(place > s, has_right)
+        return jnp.logical_and(place + s < line - 1, has_left)
+
+    def starts(way):
+        return has_right if way == 0 else has_left
+
+    def ends(way):
+        return place == 0 if way == 0 else place == line - 1
+
+    def both(fn, cond):
+        for way in range(2):
+            pl.when(cond(way))(functools.partial(fn, way))
+
+    def z_take(way, s, h):
+        def take():
+            q = source(way, s)
+            z_move(way, q, h).wait_recv()
+            if s + 1 < line:
+                pl.when(onward(way, s))(lambda: z_move(way, q, h).start())
+            y_move(q, h).start()
+            x_move(q, 0, h).start()
+            c_move(True, q, 0, h).start()
+
+        pl.when(present(way, s))(take)
+
+    def y_take(way, s, h):
+        def take():
+            q = source(way, s)
+            y_come(q, h).wait_recv()
+            x_move(q, 1, h).start()
+            c_move(True, q, 1, h).start()
+
+        pl.when(present(way, s))(take)
+
+    for h in range(split):
+        both(lambda way: z_own(way, 1, h).start(), starts)
+        y_move(place, h).start()
+        x_move(place, 0, h).start()
+    for h in range(split):
+        c_move(True, place, 0, h).start()
+    if line > 2:
+        pl.when(jnp.logical_and(place == 1, has_right))(lambda: signal(ready.at[0], (g, i + 4)))
+        pl.when(jnp.logical_and(place == line - 2, has_left))(lambda: signal(ready.at[1], (g, i - 4)))
+
+        def pass_up():
+            pl.semaphore_wait(ready.at[0], 1)
+            pl.when(has_right)(lambda: signal(ready.at[0], (g, i + 4)))
+
+        def pass_down():
+            pl.semaphore_wait(ready.at[1], 1)
+            pl.when(has_left)(lambda: signal(ready.at[1], (g, i - 4)))
+
+        pl.when(place >= 2)(pass_up)
+        pl.when(place <= line - 3)(pass_down)
+
+        def far(way):
+            for h in range(split):
+                for s in range(2, line):
+                    z_own(way, s, h).start()
+
+        both(far, ends)
+    for h in range(split):
+        for way in range(2):
+            z_take(way, 1, h)
+    for h in range(split):
+        y_come(place, h).wait_recv()
+        x_move(place, 1, h).start()
+        c_move(True, place, 1, h).start()
+    for h in range(split):
+        for s in range(2, line):
+            for way in range(2):
+                z_take(way, s, h)
+    for s in range(1, line):
+        for h in range(split):
+            for way in range(2):
+                y_take(way, s, h)
+
+    cent_copy.wait()
+    cent_wide = cent_ref[...].astype(jnp.float32)
+    half_norm = 0.5 * jnp.sum(cent_wide * cent_wide, axis=1, keepdims=True)
+
+    def score(mine, q):
+        t = 0 if mine else 1
+        group = g if mine else there
+        for side in range(2):
+            for h in range(split):
+                c_come(mine, q, side, h).wait_recv()
+        block = rows_all[group, pl.ds(q * 4, 4)].reshape(chunk, width)
+        inner = lax.dot_general(
+            cent_ref[...], block, contract_width, preferred_element_type=jnp.float32
+        )
+        logits = factor * (inner - half_norm)
+        peak = jnp.max(logits, axis=0, keepdims=True)
+        weight = jnp.exp(logits - peak)
+        weights[t, q] = weight
+        amount = jnp.sum(weight, axis=0, keepdims=True)
+        for r in range(spread):
+            peaks[t, q, r:r + 1, :] = peak[:, r * lanes:(r + 1) * lanes]
+            if mine:
+                pair[0, q, r:r + 1, :] = (peak + jnp.log(amount))[:, r * lanes:(r + 1) * lanes]
+
+    def joined(values):
+        highest = values[0]
+        for value in values[1:]:
+            highest = jnp.maximum(highest, value)
+        amount = jnp.exp(values[0] - highest)
+        for value in values[1:]:
+            amount = amount + jnp.exp(value - highest)
+        return highest + jnp.log(amount)
+
+    for j in range(line):
+        score(True, lax.rem(place + j, line))
+
+    def send(src, dst, send_sem, recv_sem, peer):
+        copy = pltpu.make_async_remote_copy(
+            src_ref=src, dst_ref=dst, send_sem=send_sem, recv_sem=recv_sem,
+            device_id=peer, device_id_type=MESH,
+        )
+        copy.start()
+        return copy
+
+    hop = send(pair.at[0], pair.at[1], q_send, q_recv, (g, core_peer))
+    hop.wait()
+    parts[0] = joined([pair[0], pair[1]])
+    hops = []
+    for k in range(2 * line - 1, 0, -1):
+        peer = lax.rem(place + k // 2, line) * 4 + lax.rem(spot + 2 * (k % 2), 4)
+        hops.append(send(parts.at[0], parts.at[k], p_send.at[k], p_recv.at[k], (g, peer)))
+
+    def x_take(q, side, h):
+        x_come(q, side, h).wait_recv()
+        c_move(False, q, side, h).start()
+
+    def x_take_if(way, s, side, h):
+        pl.when(present(way, s))(lambda: x_take(source(way, s), side, h))
+
+    for h in range(split):
+        x_take(place, 0, h)
+    for h in range(split):
+        for way in range(2):
+            x_take_if(way, 1, 0, h)
+    for h in range(split):
+        x_take(place, 1, h)
+    score(False, place)
+    for hop in hops:
+        hop.wait_recv()
+    lse = joined([parts[k] for k in range(2 * line)])
+    position = (
+        lax.broadcasted_iota(jnp.int32, lse.shape, 0) * chunk
+        + lax.broadcasted_iota(jnp.int32, lse.shape, 1) * lanes
+        + lax.broadcasted_iota(jnp.int32, lse.shape, 2)
+    )
+    valid = position < length_ref[0]
+    lses[0] = jnp.where(valid, lse, jnp.inf)
+    cross = send(lses.at[0], lses.at[1], l_send, l_recv, (there, i))
+    own_lik = jnp.where(valid, lse, 0.0)
+    count = line
+    pick = own_lik
+    for j in range(1, line):
+        pick = jnp.where(place == j, own_lik[j:j + 1], pick[0:1]) if j > 1 else jnp.where(
+            place == 1, own_lik[1:2], own_lik[0:1]
+        )
+    pick = pick[0]
+    pick = jnp.concatenate([pick[r:r + 1, :] for r in range(spread)], axis=1)
+    pick = jnp.where(spot >= 2, pick[:, 2 * row_count:], pick[:, :2 * row_count])
+    lik_out[...] = jnp.where(core == 1, pick[:, row_count:], pick[:, :row_count])
+
+    ones = jnp.ones((8, total), jnp.bfloat16)
+
+    def gather_stats(mine):
+        t = 0 if mine else 1
+        scale = jnp.exp(peaks[t] - lses[t])
+        for q in range(line):
+            for r in range(spread):
+                left = r * lanes
+                resp[:, q * chunk + left:q * chunk + left + lanes] = (
+                    weights[t, q, :, left:left + lanes] * scale[q, r:r + 1, :]
+                ).astype(jnp.bfloat16)
+        mass = lax.dot_general(ones, resp[...], contract_width, preferred_element_type=jnp.float32)
+        block = rows_all[g if mine else there].reshape(total, width)
+        weighted = lax.dot_general(resp[...], block, contract_rows, preferred_element_type=jnp.float32)
+        wide = block.astype(jnp.float32)
+        square = (wide * wide).astype(jnp.bfloat16)
+        moments = lax.dot_general(resp[...], square, contract_rows, preferred_element_type=jnp.float32)
+        return mass, weighted, moments
+
+    mass, weighted, moments = gather_stats(True)
+    cent_out[...] = weighted + prior_weight * cent_wide
+    mom_out[...] = moments + prior_weight
+    for h in range(split):
+        for s in range(2, line):
+            for way in range(2):
+                x_take_if(way, s, 0, h)
+    for s in range(1, line):
+        for h in range(split):
+            for way in range(2):
+                x_take_if(way, s, 1, h)
+    for j in range(1, line):
+        score(False, lax.rem(place + j, line))
+    cross.wait_recv()
+    mass_there, weighted, moments = gather_stats(False)
+    cent_out[...] += weighted
+    mom_out[...] += moments
+    inverse = 1.0 / (mass[0:1, :] + mass_there[0:1, :] + prior_weight)
+    inverse_out[...] = jnp.transpose(jnp.broadcast_to(inverse, (cents, cents)))
+
+    for h in range(split):
+        both(lambda way: z_own(way, 1, h).wait_send(), starts)
+
+        def far_done(way):
+            for s in range(2, line):
+                z_own(way, s, h).wait_send()
+
+        if line > 2:
+            both(far_done, ends)
+    for s in range(1, line):
+        for way in range(2):
+            if s + 1 < line:
+                def relayed():
+                    for h in range(split):
+                        z_move(way, source(way, s), h).wait_send()
+
+                pl.when(onward(way, s))(relayed)
+    for q in range(line):
+        for h in range(split):
+            y_move(q, h).wait_send()
+            for side in range(2):
+                x_move(q, side, h).wait_send()
+                c_move(True, q, side, h).wait_send()
+                c_move(False, q, side, h).wait_send()
+    for copy in hops + [cross]:
+        copy.wait_send()
+
+
+def gather_call(shards, row_count, width, cents, out_shape):
+    line = shards // 4
+    split = 4
+    total = shards * row_count
+    spread = 4 * row_count // lanes
+    vmem = pl.BlockSpec(memory_space=pltpu.VMEM)
+    hbm = pl.BlockSpec(memory_space=pltpu.HBM)
+    dma = pltpu.SemaphoreType.DMA
+    tile = (line, spread, lanes)
+    return pl.pallas_call(
+        functools.partial(gather_kernel, shards, split),
+        out_shape=out_shape,
+        in_specs=[pl.BlockSpec(memory_space=pltpu.SMEM), hbm, hbm],
+        out_specs=(vmem, vmem, vmem, vmem),
+        scratch_shapes=[
+            pltpu.VMEM((cents, width), jnp.bfloat16),
+            pltpu.VMEM((2, shards, row_count, width), jnp.bfloat16),
+            pltpu.VMEM((2, line, cents, 4 * row_count), jnp.float32),
+            pltpu.VMEM((cents, total), jnp.bfloat16),
+            pltpu.VMEM((2, *tile), jnp.float32),
+            pltpu.VMEM((2, *tile), jnp.float32),
+            pltpu.VMEM((2 * line, *tile), jnp.float32),
+            pltpu.VMEM((2, *tile), jnp.float32),
+            dma((split,)), dma, pltpu.SemaphoreType.REGULAR((2,)),
+            dma((2, line, split)), dma((line, split)), dma((line, split)),
+            dma((line, split)), dma((line, split)),
+            dma((line, 2, split)), dma((line, 2, split)),
+            dma((2, line, 2, split)), dma((2, line, 2, split)),
+            dma, dma, dma((2 * line,)), dma((2 * line,)), dma, dma,
+        ],
+        compiler_params=pltpu.CompilerParams(
+            collective_id=0, has_side_effects=True, vmem_limit_bytes=32 * 1024 * 1024
+        ),
+        name="soft_em",
+    )
+
+
 def solution(mesh):
     groups = mesh.shape["rows"]
     shards = mesh.shape["cent"]
@@ -303,36 +688,41 @@
         held = 4 * total * width + 4 * cents * total + 2 * (groups * 2 + 1) * cents * width
         steps = 2 * line - 1
         dma = pltpu.SemaphoreType.DMA
-        cent_sums, moment_sums, loglik, inverse = pl.pallas_call(
-            functools.partial(kernel, groups, shards, column_step, split),
-            out_shape=(
-                jax.ShapeDtypeStruct((cents, width), jnp.float32),
-                jax.ShapeDtypeStruct((cents, width), jnp.float32),
-                jax.ShapeDtypeStruct((1, row_count), jnp.float32),
-                jax.ShapeDtypeStruct((cents, cents), jnp.float32),
-            ),
-            in_specs=[pl.BlockSpec(memory_space=pltpu.SMEM), hbm, hbm],
-            out_specs=(vmem, vmem, vmem, vmem),
-            scratch_shapes=[
-                pltpu.VMEM((cents, width), jnp.bfloat16),
-                pltpu.VMEM((shards * split, row_count // split, width), jnp.bfloat16),
-                pltpu.VMEM((shards * split, row_count // split, width), jnp.bfloat16),
-                pltpu.VMEM((cents, total), jnp.float32),
-                pltpu.VMEM((2 + 2 * line, 2, total), jnp.float32),
-                pltpu.VMEM((groups, pieces, cents, column_step), jnp.bfloat16),
-                pltpu.VMEM((groups, 8, cents), jnp.float32),
-                dma((split,)), dma, dma((2, line, split)), dma((2, line, split)),
-                dma((steps, split)), dma((steps, split)),
-                dma((2 * steps, split)), dma((2 * steps, split)),
-                dma((2 * line,)), dma((2 * line,)),
-                dma((pieces, groups)), dma((pieces, groups)),
-                dma((groups,)), dma((groups,)),
-            ],
-            compiler_params=pltpu.CompilerParams(
-                collective_id=0, has_side_effects=True, vmem_limit_bytes=2 * held + 4 * 1024 * 1024
-            ),
-            name="soft_em",
-        )(group_length, pltpu.with_memory_space_constraint(embeddings, pltpu.HBM), pltpu.with_memory_space_constraint(centroids, pltpu.HBM))
+        out_shape = (
+            jax.ShapeDtypeStruct((cents, width), jnp.float32),
+            jax.ShapeDtypeStruct((cents, width), jnp.float32),
+            jax.ShapeDtypeStruct((1, row_count), jnp.float32),
+            jax.ShapeDtypeStruct((cents, cents), jnp.float32),
+        )
+        if groups == 2 and shards % 4 == 0 and row_count % 64 == 0 and total <= 2048:
+            call = gather_call(shards, row_count, width, cents, out_shape)
+        else:
+            call = pl.pallas_call(
+                functools.partial(sums_kernel, groups, shards, column_step, split),
+                out_shape=out_shape,
+                in_specs=[pl.BlockSpec(memory_space=pltpu.SMEM), hbm, hbm],
+                out_specs=(vmem, vmem, vmem, vmem),
+                scratch_shapes=[
+                    pltpu.VMEM((cents, width), jnp.bfloat16),
+                    pltpu.VMEM((shards * split, row_count // split, width), jnp.bfloat16),
+                    pltpu.VMEM((shards * split, row_count // split, width), jnp.bfloat16),
+                    pltpu.VMEM((cents, total), jnp.float32),
+                    pltpu.VMEM((2 + 2 * line, 2, total), jnp.float32),
+                    pltpu.VMEM((groups, pieces, cents, column_step), jnp.bfloat16),
+                    pltpu.VMEM((groups, 8, cents), jnp.float32),
+                    dma((split,)), dma, dma((2, line, split)), dma((2, line, split)),
+                    dma((steps, split)), dma((steps, split)),
+                    dma((2 * steps, split)), dma((2 * steps, split)),
+                    dma((2 * line,)), dma((2 * line,)),
+                    dma((pieces, groups)), dma((pieces, groups)),
+                    dma((groups,)), dma((groups,)),
+                ],
+                compiler_params=pltpu.CompilerParams(
+                    collective_id=0, has_side_effects=True, vmem_limit_bytes=2 * held + 4 * 1024 * 1024
+                ),
+                name="soft_em",
+            )
+        cent_sums, moment_sums, loglik, inverse = call(group_length, pltpu.with_memory_space_constraint(embeddings, pltpu.HBM), pltpu.with_memory_space_constraint(centroids, pltpu.HBM))
         new_centroids = (cent_sums * inverse[:, 0:1]).astype(jnp.bfloat16)
         new_moments = (moment_sums * inverse[:, 0:1]).astype(jnp.bfloat16)
         return new_centroids, new_moments, loglik.reshape(row_count)

time: 38.6 us -> 32.2 us (0.83)
  Pallas kernels: 35.7 us -> 29.3 us
    pallas_call x1, Pallas kernels: 35.7 us -> 29.3 us  [step(): call(group_length, pltpu.with_memory_space_constraint(embeddings, pltpu.H...]
where the time goes in v1:
time: 32.2 us; the launch traced here: 32.1 us
  Pallas kernels  29.3 us (91%)
  between operations  1.29 us (4%)
  other arithmetic  0.87 us (3%)
  local copies, waits for them, and re-layouts  0.61 us (2%)
    pallas_call x1, Pallas kernels, step(): call(group_length, pltpu.with_memory_space_constraint(embeddings, pltpu.H...  29.3 us
    convert_element_type x1, other arithmetic, step(): new_moments = (moment_sums * inverse[:, 0:1]).astype(jnp.bfloat16)  0.87 us

profile of v1, /device:TPU:0, one launch (start us, length us, event | category | flops | bytes accessed | tf_op | source)
XLA Modules:
  0.0 32.1 jit_solution(10469921827313204978)
XLA Ops:
  1.3 29.3 %soft_em.1 = (f32[128,768]{1,0:T(8,128)S(1)}, f32[128,768]{1,0:T(8,128)S(1)}, f32[1,64]{1,0:T(1,128)S(1)}, f32[128,128]{1,0:T(8,128)S(1)}) custom-call(s32[1]{0:T(128)S(6)} %copy.7.length_ref, bf16[64,768]{1,0:T(8,128)(2,1)} %emb_hbm.1, bf16[128,768]{1,0:T(8,128)(2,1)} %cent_hbm.1), custom_call_target="tpu_custom_call" | custom-call | tf_op jit(solution)/shard_map/soft_em/pallas_call | solution.py:725
  30.6 0.1 slice_reduce_fusion
  30.7 0.9 %multiply_convert_fusion = (bf16[128,768]{1,0:T(8,128)(2,1)}, bf16[128,768]{1,0:T(8,128)(2,1)}) fusion(f32[128,768]{1,0:T(8,128)S(1)} %get-tuple-element.9, f32[128]{0:T(128)S(1)} %slice_reduce_fusion, f32[128,768]{1,0:T(8,128)S(1)} %get-tuple-element.7), kind=kLoop, calls=%fused_computation | loop fusion | flops 393216 | bytes 1180160 | tf_op jit(solution)/shard_map/convert_element_type | solution.py:727
  31.6 0.5 %copy.8 = f32[64]{0:T(128)} copy(f32[64]{0:T(128)S(1)} %bitcast.1) | data formatting | bytes 512

commit v2 on v1

--- a/solution.py
+++ b/solution.py
@@ -294,7 +294,7 @@
     length_ref, emb_hbm, cent_hbm,
     cent_out, mom_out, lik_out, inverse_out,
     cent_ref, rows_all, weights, resp, peaks, pair, parts, lses,
-    own_sem, cent_sem, ready, o_send, z_send, z_recv, y_send, y_recv, x_send, x_recv,
+    own_sem, cent_sem, ready, z_send, z_recv, y_send, y_recv, x_send, x_recv,
     c_send, c_recv, q_send, q_recv, p_send, p_recv, l_send, l_recv,
 ):
     g = lax.axis_index("rows")
@@ -327,24 +327,13 @@
     pl.when(has_left)(lambda: signal(barrier, (g, i - 4)))
     for peer in [(g, y_peer), (there, i), (g, core_peer)]:
         signal(barrier, peer)
-    own = [
-        pltpu.make_async_copy(
-            emb_hbm.at[pl.ds(h * piece, piece)],
-            rows_all.at[g, i, pl.ds(h * piece, piece)], own_sem.at[h],
-        )
-        for h in range(split)
-    ]
-    for copy in own:
-        copy.start()
+    own = pltpu.make_async_copy(emb_hbm, rows_all.at[g, i], own_sem)
+    own.start()
     cent_copy = pltpu.make_async_copy(cent_hbm, cent_ref, cent_sem)
     cent_copy.start()
-    for copy in own:
-        copy.wait()
+    own.wait()
     sides = has_right.astype(jnp.int32) + has_left.astype(jnp.int32)
     pl.semaphore_wait(barrier, 3 + sides)
-
-    def slot(group, q, where, h):
-        return rows_all.at[group, q * 4 + where, pl.ds(h * piece, piece)]
 
     def move(ref, send_sem, recv_sem, peer):
         return pltpu.make_async_remote_copy(
@@ -352,45 +341,41 @@
             device_id=peer, device_id_type=MESH,
         )
 
+    def slot(group, q, where, h):
+        if h is None:
+            return rows_all.at[group, q * 4 + where]
+        return rows_all.at[group, q * 4 + where, pl.ds(h * piece, piece)]
+
+    def column(side):
+        return spot if side == 0 else y_spot
+
     def z_own(way, s, h):
         peer = (g, i + 4 * s if way == 0 else i - 4 * s)
-        return move(slot(g, place, spot, h), o_send.at[way, s, h], z_recv.at[place, h], peer)
+        return move(slot(g, place, spot, h), z_send, z_recv.at[place, h], peer)
 
     def z_move(way, q, h):
         peer = (g, i + 4 if way == 0 else i - 4)
-        return move(slot(g, q, spot, h), z_send.at[q, h], z_recv.at[q, h], peer)
+        return move(slot(g, q, spot, h), z_send, z_recv.at[q, h], peer)
 
     def y_move(q, h):
-        return move(slot(g, q, spot, h), y_send.at[q, h], y_recv.at[q, h], (g, y_peer))
-
-    def y_come(q, h):
-        return move(slot(g, q, y_spot, h), y_send.at[q, h], y_recv.at[q, h], (g, y_peer))
+        return move(slot(g, q, spot, h), y_send, y_recv.at[q], (g, y_peer))
+
+    def y_come(q):
+        return move(slot(g, q, y_spot, None), y_send, y_recv.at[q], (g, y_peer))
 
     def x_move(q, side, h):
-        where = spot if side == 0 else y_spot
-        return move(slot(g, q, where, h), x_send.at[q, side, h], x_recv.at[q, side, h], (there, i))
-
-    def x_come(q, side, h):
-        where = spot if side == 0 else y_spot
-        return move(
-            slot(there, q, where, h), x_send.at[q, side, h], x_recv.at[q, side, h], (there, i)
-        )
+        return move(slot(g, q, column(side), h), x_send, x_recv.at[q, side], (there, i))
+
+    def x_come(q, side):
+        return move(slot(there, q, column(side), None), x_send, x_recv.at[q, side], (there, i))
 
     def c_move(mine, q, side, h):
-        where = spot if side == 0 else y_spot
-        t = 0 if mine else 1
-        return move(
-            slot(g if mine else there, q, where, h),
-            c_send.at[t, q, side, h], c_recv.at[t, q, side, h], (g, core_peer),
-        )
-
-    def c_come(mine, q, side, h):
-        where = core_spot if side == 0 else core_y_spot
-        t = 0 if mine else 1
-        return move(
-            slot(g if mine else there, q, where, h),
-            c_send.at[t, q, side, h], c_recv.at[t, q, side, h], (g, core_peer),
-        )
+        ref = slot(g if mine else there, q, column(side), h)
+        return move(ref, c_send, c_recv.at[0 if mine else 1, q], (g, core_peer))
+
+    def c_come(mine, q):
+        ref = rows_all.at[g if mine else there, pl.ds(q * 4, 2)]
+        return move(ref, c_send, c_recv.at[0 if mine else 1, q], (g, core_peer))
 
     def source(way, s):
         return place - s if way == 0 else place + s
@@ -425,12 +410,12 @@
 
         pl.when(present(way, s))(take)
 
-    def y_take(way, s, h):
+    def y_take(way, s):
         def take():
             q = source(way, s)
-            y_come(q, h).wait_recv()
-            x_move(q, 1, h).start()
-            c_move(True, q, 1, h).start()
+            y_come(q).wait_recv()
+            c_move(True, q, 1, None).start()
+            x_move(q, 1, None).start()
 
         pl.when(present(way, s))(take)
 
@@ -438,8 +423,7 @@
         both(lambda way: z_own(way, 1, h).start(), starts)
         y_move(place, h).start()
         x_move(place, 0, h).start()
-    for h in range(split):
-        c_move(True, place, 0, h).start()
+    c_move(True, place, 0, None).start()
     if line > 2:
         pl.when(jnp.logical_and(place == 1, has_right))(lambda: signal(ready.at[0], (g, i + 4)))
         pl.when(jnp.logical_and(place == line - 2, has_left))(lambda: signal(ready.at[1], (g, i - 4)))
@@ -464,18 +448,16 @@
     for h in range(split):
         for way in range(2):
             z_take(way, 1, h)
-    for h in range(split):
-        y_come(place, h).wait_recv()
-        x_move(place, 1, h).start()
-        c_move(True, place, 1, h).start()
+    y_come(place).wait_recv()
+    x_move(place, 1, None).start()
+    c_move(True, place, 1, None).start()
     for h in range(split):
         for s in range(2, line):
             for way in range(2):
                 z_take(way, s, h)
     for s in range(1, line):
-        for h in range(split):
-            for way in range(2):
-                y_take(way, s, h)
+        for way in range(2):
+            y_take(way, s)
 
     cent_copy.wait()
     cent_wide = cent_ref[...].astype(jnp.float32)
@@ -484,9 +466,7 @@
     def score(mine, q):
         t = 0 if mine else 1
         group = g if mine else there
-        for side in range(2):
-            for h in range(split):
-                c_come(mine, q, side, h).wait_recv()
+        c_come(mine, q).wait_recv()
         block = rows_all[group, pl.ds(q * 4, 4)].reshape(chunk, width)
         inner = lax.dot_general(
             cent_ref[...], block, contract_width, preferred_element_type=jnp.float32
@@ -522,30 +502,28 @@
         return copy
 
     hop = send(pair.at[0], pair.at[1], q_send, q_recv, (g, core_peer))
-    hop.wait()
+    hop.wait_recv()
     parts[0] = joined([pair[0], pair[1]])
     hops = []
     for k in range(2 * line - 1, 0, -1):
         peer = lax.rem(place + k // 2, line) * 4 + lax.rem(spot + 2 * (k % 2), 4)
-        hops.append(send(parts.at[0], parts.at[k], p_send.at[k], p_recv.at[k], (g, peer)))
-
-    def x_take(q, side, h):
-        x_come(q, side, h).wait_recv()
-        c_move(False, q, side, h).start()
-
-    def x_take_if(way, s, side, h):
-        pl.when(present(way, s))(lambda: x_take(source(way, s), side, h))
-
-    for h in range(split):
-        x_take(place, 0, h)
-    for h in range(split):
-        for way in range(2):
-            x_take_if(way, 1, 0, h)
-    for h in range(split):
-        x_take(place, 1, h)
+        hops.append(send(parts.at[0], parts.at[k], p_send, p_recv, (g, peer)))
+
+    def x_take(q, side):
+        x_come(q, side).wait_recv()
+        c_move(False, q, side, None).start()
+
+    def x_take_if(way, s, side):
+        pl.when(present(way, s))(lambda: x_take(source(way, s), side))
+
+    x_take(place, 0)
+    for way in range(2):
+        x_take_if(way, 1, 0)
+    x_take(place, 1)
     score(False, place)
-    for hop in hops:
-        hop.wait_recv()
+    others = parts.at[pl.ds(1, 2 * line - 1)]
+    arrived = move(others, p_send, p_recv, (g, y_peer))
+    arrived.wait_recv()
     lse = joined([parts[k] for k in range(2 * line)])
     position = (
         lax.broadcasted_iota(jnp.int32, lse.shape, 0) * chunk
@@ -589,14 +567,12 @@
     mass, weighted, moments = gather_stats(True)
     cent_out[...] = weighted + prior_weight * cent_wide
     mom_out[...] = moments + prior_weight
-    for h in range(split):
-        for s in range(2, line):
-            for way in range(2):
-                x_take_if(way, s, 0, h)
+    for s in range(2, line):
+        for way in range(2):
+            x_take_if(way, s, 0)
     for s in range(1, line):
-        for h in range(split):
-            for way in range(2):
-                x_take_if(way, s, 1, h)
+        for way in range(2):
+            x_take_if(way, s, 1)
     for j in range(1, line):
         score(False, lax.rem(place + j, line))
     cross.wait_recv()
@@ -606,32 +582,11 @@
     inverse = 1.0 / (mass[0:1, :] + mass_there[0:1, :] + prior_weight)
     inverse_out[...] = jnp.transpose(jnp.broadcast_to(inverse, (cents, cents)))
 
-    for h in range(split):
-        both(lambda way: z_own(way, 1, h).wait_send(), starts)
-
-        def far_done(way):
-            for s in range(2, line):
-                z_own(way, s, h).wait_send()
-
-        if line > 2:
-            both(far_done, ends)
-    for s in range(1, line):
-        for way in range(2):
-            if s + 1 < line:
-                def relayed():
-                    for h in range(split):
-                        z_move(way, source(way, s), h).wait_send()
-
-                pl.when(onward(way, s))(relayed)
-    for q in range(line):
-        for h in range(split):
-            y_move(q, h).wait_send()
-            for side in range(2):
-                x_move(q, side, h).wait_send()
-                c_move(True, q, side, h).wait_send()
-                c_move(False, q, side, h).wait_send()
-    for copy in hops + [cross]:
-        copy.wait_send()
+    for sem, count in ((z_send, line - 1), (y_send, line), (x_send, 2 * line), (c_send, 4 * line)):
+        move(rows_all.at[g, pl.ds(0, count)], sem, own_sem, (g, y_peer)).wait_send()
+    arrived.wait_send()
+    hop.wait_send()
+    cross.wait_send()
 
 
 def gather_call(shards, row_count, width, cents, out_shape):
@@ -657,12 +612,9 @@
             pltpu.VMEM((2, *tile), jnp.float32),
             pltpu.VMEM((2 * line, *tile), jnp.float32),
             pltpu.VMEM((2, *tile), jnp.float32),
-            dma((split,)), dma, pltpu.SemaphoreType.REGULAR((2,)),
-            dma((2, line, split)), dma((line, split)), dma((line, split)),
-            dma((line, split)), dma((line, split)),
-            dma((line, 2, split)), dma((line, 2, split)),
-            dma((2, line, 2, split)), dma((2, line, 2, split)),
-            dma, dma, dma((2 * line,)), dma((2 * line,)), dma, dma,
+            dma, dma, pltpu.SemaphoreType.REGULAR((2,)),
+            dma, dma((line, split)), dma, dma((line,)), dma, dma((line, 2)),
+            dma, dma((2, line)), dma, dma, dma, dma, dma, dma,
         ],
         compiler_params=pltpu.CompilerParams(
             collective_id=0, has_side_effects=True, vmem_limit_bytes=32 * 1024 * 1024

time: 32.2 us -> 29.7 us (0.922)
  Pallas kernels: 29.3 us -> 26.8 us
    pallas_call x1, Pallas kernels: 29.3 us -> 26.8 us  [step(): call(group_length, pltpu.with_memory_space_constraint(embeddings, pltpu.H...]
where the time goes in v2:
time: 29.7 us; the launch traced here: 29.6 us
  Pallas kernels  26.8 us (90%)
  between operations  1.29 us (4%)
  other arithmetic  0.87 us (3%)
  local copies, waits for them, and re-layouts  0.61 us (2%)
    pallas_call x1, Pallas kernels, step(): call(group_length, pltpu.with_memory_space_constraint(embeddings, pltpu.H...  26.8 us
    convert_element_type x1, other arithmetic, step(): new_moments = (moment_sums * inverse[:, 0:1]).astype(jnp.bfloat16)  0.87 us

profile of v2, /device:TPU:0, one launch (start us, length us, event | category | flops | bytes accessed | tf_op | source)
XLA Modules:
  0.0 29.6 jit_solution(1212341495328966590)
XLA Ops:
  1.3 26.8 %soft_em.1 = (f32[128,768]{1,0:T(8,128)S(1)}, f32[128,768]{1,0:T(8,128)S(1)}, f32[1,64]{1,0:T(1,128)S(1)}, f32[128,128]{1,0:T(8,128)S(1)}) custom-call(s32[1]{0:T(128)S(6)} %copy.7.length_ref, bf16[64,768]{1,0:T(8,128)(2,1)} %emb_hbm.1, bf16[128,768]{1,0:T(8,128)(2,1)} %cent_hbm.1), custom_call_target="tpu_custom_call" | custom-call | tf_op jit(solution)/shard_map/soft_em/pallas_call | solution.py:677
  28.1 0.1 slice_reduce_fusion
  28.2 0.9 %multiply_convert_fusion = (bf16[128,768]{1,0:T(8,128)(2,1)}, bf16[128,768]{1,0:T(8,128)(2,1)}) fusion(f32[128,768]{1,0:T(8,128)S(1)} %get-tuple-element.9, f32[128]{0:T(128)S(1)} %slice_reduce_fusion, f32[128,768]{1,0:T(8,128)S(1)} %get-tuple-element.7), kind=kLoop, calls=%fused_computation | loop fusion | flops 393216 | bytes 1180160 | tf_op jit(solution)/shard_map/convert_element_type | solution.py:679
  29.0 0.5 %copy.8 = f32[64]{0:T(128)} copy(f32[64]{0:T(128)S(1)} %bitcast.1) | data formatting | bytes 512

commit v3 on v2

--- a/solution.py
+++ b/solution.py
@@ -16,6 +16,7 @@
 
 
 lanes = 128
+masked = 1e30
 
 
 def sums_kernel(
@@ -290,17 +291,17 @@
 
 
 def gather_kernel(
-    shards, split,
+    shards, split, turn, cross,
     length_ref, emb_hbm, cent_hbm,
     cent_out, mom_out, lik_out, inverse_out,
-    cent_ref, rows_all, weights, resp, peaks, pair, parts, lses,
-    own_sem, cent_sem, ready, z_send, z_recv, y_send, y_recv, x_send, x_recv,
-    c_send, c_recv, q_send, q_recv, p_send, p_recv, l_send, l_recv,
+    cents_all, rows_all, squares, weights, resp, peaks, parts, lse_ref,
+    own_sem, cent_sem, ready, know, z_send, z_recv, w_send, w_recv, y_send, y_recv, o_recv,
+    x_send, x_recv, d_recv, c_send, c_recv, k_send, k_recv, p_send, p_recv,
 ):
     g = lax.axis_index("rows")
     i = lax.axis_index("cent")
     row_count, width = emb_hbm.shape
-    cents = cent_ref.shape[0]
+    cents = cents_all.shape[1]
     total = shards * row_count
     piece = row_count // split
     line = shards // 4
@@ -329,7 +330,7 @@
         signal(barrier, peer)
     own = pltpu.make_async_copy(emb_hbm, rows_all.at[g, i], own_sem)
     own.start()
-    cent_copy = pltpu.make_async_copy(cent_hbm, cent_ref, cent_sem)
+    cent_copy = pltpu.make_async_copy(cent_hbm, cents_all.at[0], cent_sem)
     cent_copy.start()
     own.wait()
     sides = has_right.astype(jnp.int32) + has_left.astype(jnp.int32)
@@ -357,17 +358,70 @@
         peer = (g, i + 4 if way == 0 else i - 4)
         return move(slot(g, q, spot, h), z_send, z_recv.at[q, h], peer)
 
+    def low(ref, q, where):
+        return ref.at[g, q * 4 + where, pl.ds(0, cross)]
+
+    def high(ref, q, where):
+        return ref.at[g, q * 4 + where, pl.ds(cross, row_count - cross)]
+
     def y_move(q, h):
         return move(slot(g, q, spot, h), y_send, y_recv.at[q], (g, y_peer))
 
+    def y_own():
+        return move(low(rows_all, place, spot), y_send, y_recv.at[place], (g, y_peer))
+
     def y_come(q):
-        return move(slot(g, q, y_spot, None), y_send, y_recv.at[q], (g, y_peer))
-
-    def x_move(q, side, h):
-        return move(slot(g, q, column(side), h), x_send, x_recv.at[q, side], (there, i))
-
-    def x_come(q, side):
-        return move(slot(there, q, column(side), None), x_send, x_recv.at[q, side], (there, i))
+        return move(low(rows_all, q, y_spot), y_send, y_recv.at[q], (g, y_peer))
+
+    def o_own():
+        return move(high(rows_all, place, spot), w_send, o_recv, (g, y_peer))
+
+    def o_come():
+        return move(high(rows_all, place, y_spot), w_send, o_recv, (g, y_peer))
+
+    def w_move(way, q, s):
+        peer = (g, i + 4 * s if way == 0 else i - 4 * s)
+        return move(high(rows_all, q, y_spot), w_send, w_recv.at[q], peer)
+
+    def cent_move(src, k, sem, peer):
+        return pltpu.make_async_remote_copy(
+            src_ref=cent_hbm if src is None else cents_all.at[src], dst_ref=cents_all.at[k],
+            send_sem=k_send.at[sem], recv_sem=k_recv.at[k - 1], device_id=(g, peer), device_id_type=MESH,
+        )
+
+    def cent_come(k):
+        return move(cents_all.at[k], k_send.at[0], k_recv.at[k - 1], (g, y_peer))
+
+    def part(group, q, where, side):
+        rows = pl.ds(0, turn) if side == 0 else pl.ds(turn, row_count - turn)
+        return rows_all.at[group, q * 4 + where, rows]
+
+    def x_move(q, h):
+        return move(slot(g, q, spot, h), x_send, x_recv.at[q, 0], (there, i))
+
+    def x_come(q):
+        return move(slot(there, q, spot, None), x_send, x_recv.at[q, 0], (there, i))
+
+    def x_turn(q):
+        return move(part(g, q, y_spot, 0), x_send, x_recv.at[q, 1], (there, i))
+
+    def x_turned(q):
+        return move(part(there, q, y_spot, 0), x_send, x_recv.at[q, 1], (there, i))
+
+    def y_turn(q):
+        return move(part(there, q, spot, 1), y_send, d_recv.at[q], (g, y_peer))
+
+    def y_turned(q):
+        return move(part(there, q, y_spot, 1), y_send, d_recv.at[q], (g, y_peer))
+
+    def c_low(q):
+        return move(low(rows_all, q, y_spot), c_send, c_recv.at[0, q], (g, core_peer))
+
+    def c_high(q):
+        return move(high(rows_all, q, y_spot), c_send, c_recv.at[0, q], (g, core_peer))
+
+    def c_turn(q, side):
+        return move(part(there, q, y_spot, side), c_send, c_recv.at[1, q], (g, core_peer))
 
     def c_move(mine, q, side, h):
         ref = slot(g if mine else there, q, column(side), h)
@@ -382,14 +436,14 @@
 
     def present(way, s):
         return place >= s if way == 0 else place + s < line
+
+    def starts(way):
+        return has_right if way == 0 else has_left
 
     def onward(way, s):
         if way == 0:
             return jnp.logical_and(place > s, has_right)
         return jnp.logical_and(place + s < line - 1, has_left)
-
-    def starts(way):
-        return has_right if way == 0 else has_left
 
     def ends(way):
         return place == 0 if way == 0 else place == line - 1
@@ -404,26 +458,68 @@
             z_move(way, q, h).wait_recv()
             if s + 1 < line:
                 pl.when(onward(way, s))(lambda: z_move(way, q, h).start())
-            y_move(q, h).start()
-            x_move(q, 0, h).start()
+            if h * piece < cross:
+                y_move(q, h).start()
+            x_move(q, h).start()
             c_move(True, q, 0, h).start()
 
         pl.when(present(way, s))(take)
 
-    def y_take(way, s):
+    def at(way, s, fn):
+        if s == 0:
+            fn(place)
+        else:
+            pl.when(present(way, s))(lambda: fn(source(way, s)))
+
+    def y_take(q):
+        y_come(q).wait_recv()
+        x_turn(q).start()
+        c_low(q).start()
+
+    def x_take(q):
+        x_come(q).wait_recv()
+        y_turn(q).start()
+        c_move(False, q, 0, None).start()
+
+    def turn_take(q):
+        x_turned(q).wait_recv()
+        c_turn(q, 0).start()
+        y_turned(q).wait_recv()
+        c_turn(q, 1).start()
+
+    def w_take(way, s):
         def take():
             q = source(way, s)
-            y_come(q).wait_recv()
-            c_move(True, q, 1, None).start()
-            x_move(q, 1, None).start()
-
-        pl.when(present(way, s))(take)
-
+            w_move(way, q, 1).wait_recv()
+            if s + 1 < line:
+                pl.when(onward(way, s))(lambda: w_move(way, q, 1).start())
+            c_high(q).start()
+
+        if cross < row_count:
+            pl.when(present(way, s))(take)
+
+    def nth(j):
+        orders = [sorted(range(line), key=lambda q: abs(q - p)) for p in range(line)]
+        q = orders[0][j]
+        for p in range(1, line):
+            q = jnp.where(place == p, orders[p][j], q)
+        return q
+
+    near = [(way, 1) for way in range(2)]
+    far = [(way, s) for s in range(2, line) for way in range(2)]
     for h in range(split):
         both(lambda way: z_own(way, 1, h).start(), starts)
-        y_move(place, h).start()
-        x_move(place, 0, h).start()
+    if cross < row_count:
+        o_own().start()
+    cent_move(None, 2, 0, y_peer).start()
+    y_own().start()
+    x_move(place, None).start()
+    cent_move(None, 1, 1, core_peer).start()
     c_move(True, place, 0, None).start()
+
+    cube = [(g, y_peer), (there, i), (g, core_peer)]
+    for peer in cube:
+        signal(know.at[0], peer)
     if line > 2:
         pl.when(jnp.logical_and(place == 1, has_right))(lambda: signal(ready.at[0], (g, i + 4)))
         pl.when(jnp.logical_and(place == line - 2, has_left))(lambda: signal(ready.at[1], (g, i - 4)))
@@ -439,47 +535,98 @@
         pl.when(place >= 2)(pass_up)
         pl.when(place <= line - 3)(pass_down)
 
-        def far(way):
+        def far_go(way):
             for h in range(split):
                 for s in range(2, line):
                     z_own(way, s, h).start()
 
-        both(far, ends)
+        both(far_go, ends)
+
+    cent_copy.wait()
+    cent_wide = cents_all[0].astype(jnp.float32)
+    half_norm = 0.5 * jnp.sum(cent_wide * cent_wide, axis=1, keepdims=True)
+
+    def score(mine, q):
+        t = 0 if mine else 1
+        c_come(mine, q).wait_recv()
+        group = g if mine else there
+        block = rows_all[group, pl.ds(q * 4, 4)].reshape(chunk, width)
+        inner = lax.dot_general(
+            cents_all[0], block, contract_width, preferred_element_type=jnp.float32
+        )
+        logits = factor * (inner - half_norm)
+        peak = jnp.max(logits, axis=0, keepdims=True)
+        weights[t, q] = jnp.exp(logits - peak)
+        for r in range(spread):
+            peaks[t, q, r:r + 1, :] = peak[:, r * lanes:(r + 1) * lanes]
+        wide = block.astype(jnp.float32)
+        squares[group, pl.ds(q * 4, 4)] = (wide * wide).astype(jnp.bfloat16).reshape(
+            4, row_count, width
+        )
+
+    def partial_lse(all_half, q):
+        block = rows_all[g, q * 4 + spot]
+        inner = lax.dot_general(
+            cents_all[...].reshape(4 * cents, width), block, contract_width,
+            preferred_element_type=jnp.float32,
+        )
+        logits = factor * (inner - all_half)
+        peak = jnp.max(logits, axis=0, keepdims=True)
+        value = peak + jnp.log(jnp.sum(jnp.exp(logits - peak), axis=0, keepdims=True))
+        row = (q * 4 + spot) * row_count + lax.broadcasted_iota(jnp.int32, value.shape, 1)
+        parts[g, i, pl.ds(q, 1), :] = jnp.where(row < length_ref[0], value, masked)
+
     for h in range(split):
         for way in range(2):
             z_take(way, 1, h)
-    y_come(place).wait_recv()
-    x_move(place, 1, None).start()
-    c_move(True, place, 1, None).start()
-    for h in range(split):
-        for s in range(2, line):
-            for way in range(2):
-                z_take(way, s, h)
-    for s in range(1, line):
-        for way in range(2):
-            y_take(way, s)
-
-    cent_copy.wait()
-    cent_wide = cent_ref[...].astype(jnp.float32)
-    half_norm = 0.5 * jnp.sum(cent_wide * cent_wide, axis=1, keepdims=True)
-
-    def score(mine, q):
-        t = 0 if mine else 1
-        group = g if mine else there
-        c_come(mine, q).wait_recv()
-        block = rows_all[group, pl.ds(q * 4, 4)].reshape(chunk, width)
-        inner = lax.dot_general(
-            cent_ref[...], block, contract_width, preferred_element_type=jnp.float32
-        )
-        logits = factor * (inner - half_norm)
-        peak = jnp.max(logits, axis=0, keepdims=True)
-        weight = jnp.exp(logits - peak)
-        weights[t, q] = weight
-        amount = jnp.sum(weight, axis=0, keepdims=True)
-        for r in range(spread):
-            peaks[t, q, r:r + 1, :] = peak[:, r * lanes:(r + 1) * lanes]
-            if mine:
-                pair[0, q, r:r + 1, :] = (peak + jnp.log(amount))[:, r * lanes:(r + 1) * lanes]
+    pl.semaphore_wait(know.at[0], 3)
+    for peer in cube:
+        signal(know.at[1], peer)
+    if cross < row_count:
+        o_come().wait_recv()
+        both(lambda way: w_move(way, place, 1).start(), starts)
+
+        def w_far(way):
+            for s in range(2, line):
+                w_move(way, place, s).start()
+
+        if line > 2:
+            both(w_far, ends)
+        c_high(place).start()
+    for h in range(split // 2):
+        for way, s in far:
+            z_take(way, s, h)
+    pl.semaphore_wait(know.at[1], 3)
+    for q in range(1, line):
+        signal(know.at[2], (g, lax.rem(place + q, line) * 4 + spot))
+    cent_come(2).wait_recv()
+    cent_move(2, 3, 2, core_peer).start()
+    y_take(place)
+    x_take(place)
+    for k in (1, 3):
+        cent_come(k).wait_recv()
+    wide = cents_all[...].reshape(4 * cents, width).astype(jnp.float32)
+    all_half = 0.5 * jnp.sum(wide * wide, axis=1, keepdims=True)
+    partial_lse(all_half, place)
+    for way, s in near:
+        at(way, s, functools.partial(partial_lse, all_half))
+    for h in range(split // 2, split):
+        for way, s in far:
+            z_take(way, s, h)
+    for way, s in far:
+        at(way, s, functools.partial(partial_lse, all_half))
+
+    pl.semaphore_wait(know.at[2], line - 1)
+    mine_part = parts.at[g, i]
+    for k in range(shards - 1, -1, -1):
+        peer = lax.rem(i + k, shards)
+        for group, t in ((there, 1), (g, 0)):
+            if k > 0 or t:
+                move_to = pltpu.make_async_remote_copy(
+                    src_ref=mine_part, dst_ref=mine_part, send_sem=p_send.at[t],
+                    recv_sem=p_recv.at[t], device_id=(group, peer), device_id_type=MESH,
+                )
+                move_to.start()
 
     def joined(values):
         highest = values[0]
@@ -490,131 +637,145 @@
             amount = amount + jnp.exp(value - highest)
         return highest + jnp.log(amount)
 
-    for j in range(line):
-        score(True, lax.rem(place + j, line))
-
-    def send(src, dst, send_sem, recv_sem, peer):
-        copy = pltpu.make_async_remote_copy(
-            src_ref=src, dst_ref=dst, send_sem=send_sem, recv_sem=recv_sem,
-            device_id=peer, device_id_type=MESH,
-        )
-        copy.start()
-        return copy
-
-    hop = send(pair.at[0], pair.at[1], q_send, q_recv, (g, core_peer))
-    hop.wait_recv()
-    parts[0] = joined([pair[0], pair[1]])
-    hops = []
-    for k in range(2 * line - 1, 0, -1):
-        peer = lax.rem(place + k // 2, line) * 4 + lax.rem(spot + 2 * (k % 2), 4)
-        hops.append(send(parts.at[0], parts.at[k], p_send, p_recv, (g, peer)))
-
-    def x_take(q, side):
-        x_come(q, side).wait_recv()
-        c_move(False, q, side, None).start()
-
-    def x_take_if(way, s, side):
-        pl.when(present(way, s))(lambda: x_take(source(way, s), side))
-
-    x_take(place, 0)
-    for way in range(2):
-        x_take_if(way, 1, 0)
-    x_take(place, 1)
-    score(False, place)
-    others = parts.at[pl.ds(1, 2 * line - 1)]
-    arrived = move(others, p_send, p_recv, (g, y_peer))
-    arrived.wait_recv()
-    lse = joined([parts[k] for k in range(2 * line)])
-    position = (
-        lax.broadcasted_iota(jnp.int32, lse.shape, 0) * chunk
-        + lax.broadcasted_iota(jnp.int32, lse.shape, 1) * lanes
-        + lax.broadcasted_iota(jnp.int32, lse.shape, 2)
+    def move_parts(group, count, k):
+        return move(parts.at[group, pl.ds(0, count)], p_send.at[k], p_recv.at[k], (g, y_peer))
+
+    def whole_lse(group):
+        return [joined([parts[group, p * 4 + w] for p in range(line)]) for w in range(4)]
+
+    ones = jnp.ones((8, total), jnp.bfloat16)
+
+    def weigh(t, q, place_in_resp):
+        for r in range(spread):
+            left = r * lanes
+            scale = jnp.exp(peaks[t, q, r:r + 1, :] - lse_ref[t, r, pl.ds(q, 1), :])
+            resp[:, place_in_resp * chunk + left:place_in_resp * chunk + left + lanes] = (
+                weights[t, q, :, left:left + lanes] * scale
+            ).astype(jnp.bfloat16)
+
+    def times(left, right):
+        return lax.dot_general(left, right, contract_rows, preferred_element_type=jnp.float32)
+
+    def mass_of(block):
+        return lax.dot_general(
+            ones[:, :block.shape[1]], block, contract_width, preferred_element_type=jnp.float32
+        )
+
+    def keep_lse(t, lse):
+        for r in range(spread):
+            lse_ref[t, r] = jnp.concatenate([lse[2 * r], lse[2 * r + 1]], axis=1)
+
+    def add_there(orders):
+        mass = 0.0
+        weighted = cent_out[...]
+        moments = mom_out[...]
+        for n, q in enumerate(orders):
+            weigh(1, q, n)
+            block = resp[:, n * chunk:(n + 1) * chunk]
+            mass = mass + mass_of(block)
+            weighted = weighted + times(block, rows_all[there, pl.ds(q * 4, 4)].reshape(chunk, width))
+            moments = moments + times(block, squares[there, pl.ds(q * 4, 4)].reshape(chunk, width))
+        cent_out[...] = weighted
+        mom_out[...] = moments
+        return mass
+
+    places = [place] + [nth(j) for j in range(1, line)]
+    half = line // 2
+    for way, s in near:
+        w_take(way, s)
+    for j in range(1, half):
+        y_take(places[j])
+        x_take(places[j])
+    score(True, place)
+    for way, s in far:
+        w_take(way, s)
+    for j in range(half, line):
+        y_take(places[j])
+        x_take(places[j])
+    for j in range(1, half):
+        score(True, places[j])
+    for j in range(half):
+        turn_take(places[j])
+    for j in range(half, line):
+        score(True, places[j])
+
+    move_parts(g, shards - 1, 0).wait_recv()
+    lse = whole_lse(g)
+    keep_lse(0, lse)
+    for q in range(line):
+        weigh(0, q, q)
+    mass = mass_of(resp[...])
+    cent_out[...] = prior_weight * cent_wide + times(
+        resp[...], rows_all[g].reshape(total, width)
     )
-    valid = position < length_ref[0]
-    lses[0] = jnp.where(valid, lse, jnp.inf)
-    cross = send(lses.at[0], lses.at[1], l_send, l_recv, (there, i))
-    own_lik = jnp.where(valid, lse, 0.0)
-    count = line
-    pick = own_lik
-    for j in range(1, line):
-        pick = jnp.where(place == j, own_lik[j:j + 1], pick[0:1]) if j > 1 else jnp.where(
-            place == 1, own_lik[1:2], own_lik[0:1]
-        )
-    pick = pick[0]
-    pick = jnp.concatenate([pick[r:r + 1, :] for r in range(spread)], axis=1)
-    pick = jnp.where(spot >= 2, pick[:, 2 * row_count:], pick[:, :2 * row_count])
-    lik_out[...] = jnp.where(core == 1, pick[:, row_count:], pick[:, :row_count])
-
-    ones = jnp.ones((8, total), jnp.bfloat16)
-
-    def gather_stats(mine):
-        t = 0 if mine else 1
-        scale = jnp.exp(peaks[t] - lses[t])
-        for q in range(line):
-            for r in range(spread):
-                left = r * lanes
-                resp[:, q * chunk + left:q * chunk + left + lanes] = (
-                    weights[t, q, :, left:left + lanes] * scale[q, r:r + 1, :]
-                ).astype(jnp.bfloat16)
-        mass = lax.dot_general(ones, resp[...], contract_width, preferred_element_type=jnp.float32)
-        block = rows_all[g if mine else there].reshape(total, width)
-        weighted = lax.dot_general(resp[...], block, contract_rows, preferred_element_type=jnp.float32)
-        wide = block.astype(jnp.float32)
-        square = (wide * wide).astype(jnp.bfloat16)
-        moments = lax.dot_general(resp[...], square, contract_rows, preferred_element_type=jnp.float32)
-        return mass, weighted, moments
-
-    mass, weighted, moments = gather_stats(True)
-    cent_out[...] = weighted + prior_weight * cent_wide
-    mom_out[...] = moments + prior_weight
-    for s in range(2, line):
-        for way in range(2):
-            x_take_if(way, s, 0)
-    for s in range(1, line):
-        for way in range(2):
-            x_take_if(way, s, 1)
-    for j in range(1, line):
-        score(False, lax.rem(place + j, line))
-    cross.wait_recv()
-    mass_there, weighted, moments = gather_stats(False)
-    cent_out[...] += weighted
-    mom_out[...] += moments
-    inverse = 1.0 / (mass[0:1, :] + mass_there[0:1, :] + prior_weight)
+    mom_out[...] = prior_weight + times(resp[...], squares[g].reshape(total, width))
+    for j in range(half):
+        score(False, places[j])
+    move_parts(there, shards, 1).wait_recv()
+    keep_lse(1, whole_lse(there))
+    mass = mass + add_there(places[:half])
+    for j in range(half, line):
+        turn_take(places[j])
+    pick = lse[0]
+    for w in range(1, 4):
+        pick = jnp.where(spot == w, lse[w], pick)
+    own_lik = pick[0:1]
+    for q in range(1, line):
+        own_lik = jnp.where(place == q, pick[q:q + 1], own_lik)
+    row = i * row_count + lax.broadcasted_iota(jnp.int32, own_lik.shape, 1)
+    lik_out[...] = jnp.where(row < length_ref[0], own_lik, 0.0)
+    for j in range(half, line):
+        score(False, places[j])
+    mass = mass + add_there(places[half:])
+    inverse = 1.0 / (mass[0:1, :] + prior_weight)
     inverse_out[...] = jnp.transpose(jnp.broadcast_to(inverse, (cents, cents)))
 
-    for sem, count in ((z_send, line - 1), (y_send, line), (x_send, 2 * line), (c_send, 4 * line)):
-        move(rows_all.at[g, pl.ds(0, count)], sem, own_sem, (g, y_peer)).wait_send()
-    arrived.wait_send()
-    hop.wait_send()
-    cross.wait_send()
+    def drain(sem, count):
+        step = max(b for b in range(piece, row_count + 1, piece) if count % b == 0)
+        rows = rows_all.at[g, pl.ds(0, count // step), pl.ds(0, step)]
+        move(rows, sem, own_sem, (g, y_peer)).wait_send()
+
+    drain(z_send, (line - 1) * row_count)
+    drain(y_send, line * (cross + row_count - turn))
+    drain(x_send, line * (row_count + turn))
+    drain(c_send, 4 * line * row_count)
+    if cross < row_count:
+        drain(w_send, line * (row_count - cross))
+    for k in range(3):
+        move(cents_all.at[1], k_send.at[k], own_sem, (g, y_peer)).wait_send()
+    move_parts(g, shards - 1, 0).wait_send()
+    move_parts(there, shards, 1).wait_send()
 
 
 def gather_call(shards, row_count, width, cents, out_shape):
     line = shards // 4
     split = 4
+    cross = row_count // 2
+    turn = row_count // 2
     total = shards * row_count
     spread = 4 * row_count // lanes
     vmem = pl.BlockSpec(memory_space=pltpu.VMEM)
     hbm = pl.BlockSpec(memory_space=pltpu.HBM)
     dma = pltpu.SemaphoreType.DMA
-    tile = (line, spread, lanes)
+    regular = pltpu.SemaphoreType.REGULAR
     return pl.pallas_call(
-        functools.partial(gather_kernel, shards, split),
+        functools.partial(gather_kernel, shards, split, turn, cross),
         out_shape=out_shape,
         in_specs=[pl.BlockSpec(memory_space=pltpu.SMEM), hbm, hbm],
         out_specs=(vmem, vmem, vmem, vmem),
         scratch_shapes=[
-            pltpu.VMEM((cents, width), jnp.bfloat16),
+            pltpu.VMEM((4, cents, width), jnp.bfloat16),
+            pltpu.VMEM((2, shards, row_count, width), jnp.bfloat16),
             pltpu.VMEM((2, shards, row_count, width), jnp.bfloat16),
             pltpu.VMEM((2, line, cents, 4 * row_count), jnp.float32),
             pltpu.VMEM((cents, total), jnp.bfloat16),
-            pltpu.VMEM((2, *tile), jnp.float32),
-            pltpu.VMEM((2, *tile), jnp.float32),
-            pltpu.VMEM((2 * line, *tile), jnp.float32),
-            pltpu.VMEM((2, *tile), jnp.float32),
-            dma, dma, pltpu.SemaphoreType.REGULAR((2,)),
-            dma, dma((line, split)), dma, dma((line,)), dma, dma((line, 2)),
-            dma, dma((2, line)), dma, dma, dma, dma, dma, dma,
+            pltpu.VMEM((2, line, spread, lanes), jnp.float32),
+            pltpu.VMEM((2, shards, line, row_count), jnp.float32),
+            pltpu.VMEM((2, spread, line, lanes), jnp.float32),
+            dma, dma, regular((2,)), regular((3,)),
+            dma, dma((line, split)), dma, dma((line,)), dma, dma((line,)), dma,
+            dma, dma((line, 2)), dma((line,)), dma, dma((2, line)), dma((3,)), dma((3,)),
+            dma((2,)), dma((2,)),
         ],
         compiler_params=pltpu.CompilerParams(
             collective_id=0, has_side_effects=True, vmem_limit_bytes=32 * 1024 * 1024
@@ -646,7 +807,7 @@
             jax.ShapeDtypeStruct((1, row_count), jnp.float32),
             jax.ShapeDtypeStruct((cents, cents), jnp.float32),
         )
-        if groups == 2 and shards % 4 == 0 and row_count % 64 == 0 and total <= 2048:
+        if groups == 2 and shards % 4 == 0 and shards > 4 and row_count % 64 == 0 and total <= 2048:
             call = gather_call(shards, row_count, width, cents, out_shape)
         else:
             call = pl.pallas_call(

time: 29.7 us -> 28.8 us (0.970)
  Pallas kernels: 26.8 us -> 25.9 us
    pallas_call x1, Pallas kernels: 26.8 us -> 25.9 us  [step(): call(group_length, pltpu.with_memory_space_constraint(embeddings, pltpu.H...]
where the time goes in v3:
time: 28.8 us; the launch traced here: 28.7 us
  Pallas kernels  25.9 us (90%)
  between operations  1.29 us (4%)
  other arithmetic  0.87 us (3%)
  local copies, waits for them, and re-layouts  0.61 us (2%)
    pallas_call x1, Pallas kernels, step(): call(group_length, pltpu.with_memory_space_constraint(embeddings, pltpu.H...  25.9 us
    convert_element_type x1, other arithmetic, step(): new_moments = (moment_sums * inverse[:, 0:1]).astype(jnp.bfloat16)  0.87 us

profile of v3, /device:TPU:0, one launch (start us, length us, event | category | flops | bytes accessed | tf_op | source)
XLA Modules:
  0.0 28.7 jit_solution(187133487268582775)
XLA Ops:
  1.3 25.9 %soft_em.1 = (f32[128,768]{1,0:T(8,128)S(1)}, f32[128,768]{1,0:T(8,128)S(1)}, f32[1,64]{1,0:T(1,128)S(1)}, f32[128,128]{1,0:T(8,128)S(1)}) custom-call(s32[1]{0:T(128)S(6)} %copy.7.length_ref, bf16[64,768]{1,0:T(8,128)(2,1)} %emb_hbm.1, bf16[128,768]{1,0:T(8,128)(2,1)} %cent_hbm.1), custom_call_target="tpu_custom_call" | custom-call | tf_op jit(solution)/shard_map/soft_em/pallas_call | solution.py:838
  27.2 0.1 slice_reduce_fusion
  27.3 0.9 %multiply_convert_fusion = (bf16[128,768]{1,0:T(8,128)(2,1)}, bf16[128,768]{1,0:T(8,128)(2,1)}) fusion(f32[128,768]{1,0:T(8,128)S(1)} %get-tuple-element.9, f32[128]{0:T(128)S(1)} %slice_reduce_fusion, f32[128,768]{1,0:T(8,128)S(1)} %get-tuple-element.7), kind=kLoop, calls=%fused_computation | loop fusion | flops 393216 | bytes 1180160 | tf_op jit(solution)/shard_map/convert_element_type | solution.py:840
  28.1 0.5 %copy.8 = f32[64]{0:T(128)} copy(f32[64]{0:T(128)S(1)} %bitcast.1) | data formatting | bytes 512

commit v4 on v3

--- a/solution.py
+++ b/solution.py
@@ -291,7 +291,7 @@
 
 
 def gather_kernel(
-    shards, split, turn, cross,
+    shards, split, turn, cross, steps,
     length_ref, emb_hbm, cent_hbm,
     cent_out, mom_out, lik_out, inverse_out,
     cents_all, rows_all, squares, weights, resp, peaks, parts, lse_ref,
@@ -397,16 +397,23 @@
         return rows_all.at[group, q * 4 + where, rows]
 
     def x_move(q, h):
-        return move(slot(g, q, spot, h), x_send, x_recv.at[q, 0], (there, i))
-
-    def x_come(q):
-        return move(slot(there, q, spot, None), x_send, x_recv.at[q, 0], (there, i))
+        side = 0 if h * piece < turn else 1
+        return move(slot(g, q, spot, h), x_send, x_recv.at[q, side], (there, i))
+
+    def x_own(side):
+        return move(part(g, place, spot, side), x_send, x_recv.at[place, side], (there, i))
+
+    def x_come(q, side):
+        return move(part(there, q, spot, side), x_send, x_recv.at[q, side], (there, i))
+
+    def c_part(q, side):
+        return move(part(there, q, spot, side), c_send, c_recv.at[1, q], (g, core_peer))
 
     def x_turn(q):
-        return move(part(g, q, y_spot, 0), x_send, x_recv.at[q, 1], (there, i))
+        return move(part(g, q, y_spot, 0), x_send, x_recv.at[q, 2], (there, i))
 
     def x_turned(q):
-        return move(part(there, q, y_spot, 0), x_send, x_recv.at[q, 1], (there, i))
+        return move(part(there, q, y_spot, 0), x_send, x_recv.at[q, 2], (there, i))
 
     def y_turn(q):
         return move(part(there, q, spot, 1), y_send, d_recv.at[q], (g, y_peer))
@@ -476,16 +483,15 @@
         x_turn(q).start()
         c_low(q).start()
 
-    def x_take(q):
-        x_come(q).wait_recv()
-        y_turn(q).start()
-        c_move(False, q, 0, None).start()
-
-    def turn_take(q):
-        x_turned(q).wait_recv()
-        c_turn(q, 0).start()
-        y_turned(q).wait_recv()
-        c_turn(q, 1).start()
+    def x_take(q, side):
+        x_come(q, side).wait_recv()
+        if side == 1:
+            y_turn(q).start()
+        c_part(q, side).start()
+
+    def turn_take(q, side):
+        (y_turned if side else x_turned)(q).wait_recv()
+        c_turn(q, side).start()
 
     def w_take(way, s):
         def take():
@@ -511,9 +517,10 @@
         both(lambda way: z_own(way, 1, h).start(), starts)
     if cross < row_count:
         o_own().start()
+    y_own().start()
     cent_move(None, 2, 0, y_peer).start()
-    y_own().start()
-    x_move(place, None).start()
+    x_own(0).start()
+    x_own(1).start()
     cent_move(None, 1, 1, core_peer).start()
     c_move(True, place, 0, None).start()
 
@@ -576,58 +583,6 @@
         row = (q * 4 + spot) * row_count + lax.broadcasted_iota(jnp.int32, value.shape, 1)
         parts[g, i, pl.ds(q, 1), :] = jnp.where(row < length_ref[0], value, masked)
 
-    for h in range(split):
-        for way in range(2):
-            z_take(way, 1, h)
-    pl.semaphore_wait(know.at[0], 3)
-    for peer in cube:
-        signal(know.at[1], peer)
-    if cross < row_count:
-        o_come().wait_recv()
-        both(lambda way: w_move(way, place, 1).start(), starts)
-
-        def w_far(way):
-            for s in range(2, line):
-                w_move(way, place, s).start()
-
-        if line > 2:
-            both(w_far, ends)
-        c_high(place).start()
-    for h in range(split // 2):
-        for way, s in far:
-            z_take(way, s, h)
-    pl.semaphore_wait(know.at[1], 3)
-    for q in range(1, line):
-        signal(know.at[2], (g, lax.rem(place + q, line) * 4 + spot))
-    cent_come(2).wait_recv()
-    cent_move(2, 3, 2, core_peer).start()
-    y_take(place)
-    x_take(place)
-    for k in (1, 3):
-        cent_come(k).wait_recv()
-    wide = cents_all[...].reshape(4 * cents, width).astype(jnp.float32)
-    all_half = 0.5 * jnp.sum(wide * wide, axis=1, keepdims=True)
-    partial_lse(all_half, place)
-    for way, s in near:
-        at(way, s, functools.partial(partial_lse, all_half))
-    for h in range(split // 2, split):
-        for way, s in far:
-            z_take(way, s, h)
-    for way, s in far:
-        at(way, s, functools.partial(partial_lse, all_half))
-
-    pl.semaphore_wait(know.at[2], line - 1)
-    mine_part = parts.at[g, i]
-    for k in range(shards - 1, -1, -1):
-        peer = lax.rem(i + k, shards)
-        for group, t in ((there, 1), (g, 0)):
-            if k > 0 or t:
-                move_to = pltpu.make_async_remote_copy(
-                    src_ref=mine_part, dst_ref=mine_part, send_sem=p_send.at[t],
-                    recv_sem=p_recv.at[t], device_id=(group, peer), device_id_type=MESH,
-                )
-                move_to.start()
-
     def joined(values):
         highest = values[0]
         for value in values[1:]:
@@ -670,8 +625,8 @@
         weighted = cent_out[...]
         moments = mom_out[...]
         for n, q in enumerate(orders):
-            weigh(1, q, n)
-            block = resp[:, n * chunk:(n + 1) * chunk]
+            weigh(1, q, line + n)
+            block = resp[:, total + n * chunk:total + (n + 1) * chunk]
             mass = mass + mass_of(block)
             weighted = weighted + times(block, rows_all[there, pl.ds(q * 4, 4)].reshape(chunk, width))
             moments = moments + times(block, squares[there, pl.ds(q * 4, 4)].reshape(chunk, width))
@@ -680,53 +635,131 @@
         return mass
 
     places = [place] + [nth(j) for j in range(1, line)]
-    half = line // 2
-    for way, s in near:
-        w_take(way, s)
-    for j in range(1, half):
-        y_take(places[j])
-        x_take(places[j])
-    score(True, place)
-    for way, s in far:
-        w_take(way, s)
-    for j in range(half, line):
-        y_take(places[j])
-        x_take(places[j])
-    for j in range(1, half):
-        score(True, places[j])
-    for j in range(half):
-        turn_take(places[j])
-    for j in range(half, line):
-        score(True, places[j])
-
-    move_parts(g, shards - 1, 0).wait_recv()
-    lse = whole_lse(g)
-    keep_lse(0, lse)
-    for q in range(line):
-        weigh(0, q, q)
-    mass = mass_of(resp[...])
-    cent_out[...] = prior_weight * cent_wide + times(
-        resp[...], rows_all[g].reshape(total, width)
-    )
-    mom_out[...] = prior_weight + times(resp[...], squares[g].reshape(total, width))
-    for j in range(half):
+    state = {"half": None, "mass": None, "lse": None, "told": False, "ready": [], "there": False, "moments": False}
+
+    def near_rows(h):
+        for way, s in near:
+            z_take(way, s, h)
+
+    def far_rows(h):
+        for way, s in far:
+            z_take(way, s, h)
+
+    def other_column(_):
+        if cross == row_count:
+            return
+        o_come().wait_recv()
+        both(lambda way: w_move(way, place, 1).start(), starts)
+
+        def w_far(way):
+            for s in range(2, line):
+                w_move(way, place, s).start()
+
+        if line > 2:
+            both(w_far, ends)
+        c_high(place).start()
+
+    def tell(_):
+        pl.semaphore_wait(know.at[0], 3)
+        for peer in cube:
+            signal(know.at[1], peer)
+
+    def tell_line(_):
+        pl.semaphore_wait(know.at[1], 3)
+        for q in range(1, line):
+            signal(know.at[2], (g, lax.rem(place + q, line) * 4 + spot))
+
+    def cents_out(_):
+        cent_move(None, 2, 0, y_peer).start()
+
+    def half_of(k):
+        wide = cents_all[k].astype(jnp.float32)
+        return 0.5 * jnp.sum(wide * wide, axis=1, keepdims=True)
+
+    def cents_in(_):
+        cent_come(2).wait_recv()
+        cent_move(2, 3, 2, core_peer).start()
+        cent_come(1).wait_recv()
+        state["halves"] = [half_norm, half_of(1), half_of(2)]
+
+    def cents_ready(_):
+        cent_come(3).wait_recv()
+        state["half"] = jnp.concatenate([*state["halves"], half_of(3)], axis=0)
+
+    def normaliser(k):
+        if k == 0:
+            partial_lse(state["half"], place)
+        for way, s in (near, far)[k - 1] if k else ():
+            at(way, s, functools.partial(partial_lse, state["half"]))
+
+    def send_parts(_):
+        pl.semaphore_wait(know.at[2], line - 1)
+        mine_part = parts.at[g, i]
+        for k in range(shards - 1, -1, -1):
+            peer = lax.rem(i + k, shards)
+            for group, t in ((there, 1), (g, 0)):
+                if k > 0 or t:
+                    pltpu.make_async_remote_copy(
+                        src_ref=mine_part, dst_ref=mine_part, send_sem=p_send.at[t],
+                        recv_sem=p_recv.at[t], device_id=(group, peer), device_id_type=MESH,
+                    ).start()
+
+    def crossed(k):
+        for way, s in (near, far)[k]:
+            w_take(way, s)
+
+    def own_sums(_):
+        move_parts(g, shards - 1, 0).wait_recv()
+        lse = whole_lse(g)
+        keep_lse(0, lse)
+        for q in range(line):
+            weigh(0, q, q)
+        state["mass"] = mass_of(resp[:, :total])
+        cent_out[...] = prior_weight * cent_wide + times(
+            resp[:, :total], rows_all[g].reshape(total, width)
+        )
+        state["lse"] = lse
+
+    def own_moments(_):
+        mom_out[...] = prior_weight + times(resp[:, :total], squares[g].reshape(total, width))
+        state["moments"] = True
+
+    def score_there(j):
         score(False, places[j])
-    move_parts(there, shards, 1).wait_recv()
-    keep_lse(1, whole_lse(there))
-    mass = mass + add_there(places[:half])
-    for j in range(half, line):
-        turn_take(places[j])
-    pick = lse[0]
-    for w in range(1, 4):
-        pick = jnp.where(spot == w, lse[w], pick)
-    own_lik = pick[0:1]
-    for q in range(1, line):
-        own_lik = jnp.where(place == q, pick[q:q + 1], own_lik)
-    row = i * row_count + lax.broadcasted_iota(jnp.int32, own_lik.shape, 1)
-    lik_out[...] = jnp.where(row < length_ref[0], own_lik, 0.0)
-    for j in range(half, line):
-        score(False, places[j])
-    mass = mass + add_there(places[half:])
+        state["ready"].append(places[j])
+
+    def sums_there(_):
+        if not state["moments"] or not state["ready"]:
+            return
+        if not state["there"]:
+            move_parts(there, shards, 1).wait_recv()
+            keep_lse(1, whole_lse(there))
+            state["there"] = True
+        state["mass"] = state["mass"] + add_there(state["ready"])
+        state["ready"] = []
+
+    def write_lik(_):
+        lse = state["lse"]
+        pick = lse[0]
+        for w in range(1, 4):
+            pick = jnp.where(spot == w, lse[w], pick)
+        own_lik = pick[0:1]
+        for q in range(1, line):
+            own_lik = jnp.where(place == q, pick[q:q + 1], own_lik)
+        row = i * row_count + lax.broadcasted_iota(jnp.int32, own_lik.shape, 1)
+        lik_out[...] = jnp.where(row < length_ref[0], own_lik, 0.0)
+
+    acts = {
+        "N": near_rows, "Z": far_rows, "O": other_column, "E": tell, "F": tell_line,
+        "K": cents_out, "I": cents_in, "C": cents_ready, "A": normaliser, "L": send_parts,
+        "W": crossed, "Y": lambda j: y_take(places[j]), "H": lambda j: x_take(places[j], 1),
+        "G": lambda j: x_take(places[j], 0), "T": lambda j: turn_take(places[j], 0),
+        "D": lambda j: turn_take(places[j], 1), "S": lambda j: score(True, places[j]),
+        "s": score_there, "R": own_sums, "M": own_moments, "r": sums_there, "l": write_lik,
+    }
+    for step in steps:
+        acts[step[0]](int(step[1:] or 0))
+    mass = state["mass"]
     inverse = 1.0 / (mass[0:1, :] + prior_weight)
     inverse_out[...] = jnp.transpose(jnp.broadcast_to(inverse, (cents, cents)))
 
@@ -747,11 +780,25 @@
     move_parts(there, shards, 1).wait_send()
 
 
+schedule = (
+    "N0", "N1", "Y0", "E", "O", "N2", "S0", "G1", "H0", "N3", "G0", "Z1",
+    "Z0", "F", "I", "T0", "Z2", "W0", "H1", "Z3", "Y1", "C", "A0", "A1",
+    "A2", "Y2", "L", "H2", "Y3", "G2", "D0", "H3", "W1", "S1", "D1", "s0",
+    "T1", "S3", "G3", "S2", "s1", "R", "T2", "D2", "M", "T3", "D3", "r",
+    "s2", "l", "s3", "r",
+)
+
+
+def gather_steps(line, split):
+    assert line == 4 and split == 4
+    return schedule
+
+
 def gather_call(shards, row_count, width, cents, out_shape):
     line = shards // 4
     split = 4
-    cross = row_count // 2
-    turn = row_count // 2
+    cross = row_count * 2 // 4
+    turn = row_count * 2 // 4
     total = shards * row_count
     spread = 4 * row_count // lanes
     vmem = pl.BlockSpec(memory_space=pltpu.VMEM)
@@ -759,7 +806,7 @@
     dma = pltpu.SemaphoreType.DMA
     regular = pltpu.SemaphoreType.REGULAR
     return pl.pallas_call(
-        functools.partial(gather_kernel, shards, split, turn, cross),
+        functools.partial(gather_kernel, shards, split, turn, cross, gather_steps(line, split)),
         out_shape=out_shape,
         in_specs=[pl.BlockSpec(memory_space=pltpu.SMEM), hbm, hbm],
         out_specs=(vmem, vmem, vmem, vmem),
@@ -768,13 +815,13 @@
             pltpu.VMEM((2, shards, row_count, width), jnp.bfloat16),
             pltpu.VMEM((2, shards, row_count, width), jnp.bfloat16),
             pltpu.VMEM((2, line, cents, 4 * row_count), jnp.float32),
-            pltpu.VMEM((cents, total), jnp.bfloat16),
+            pltpu.VMEM((cents, 2 * total), jnp.bfloat16),
             pltpu.VMEM((2, line, spread, lanes), jnp.float32),
             pltpu.VMEM((2, shards, line, row_count), jnp.float32),
             pltpu.VMEM((2, spread, line, lanes), jnp.float32),
             dma, dma, regular((2,)), regular((3,)),
             dma, dma((line, split)), dma, dma((line,)), dma, dma((line,)), dma,
-            dma, dma((line, 2)), dma((line,)), dma, dma((2, line)), dma((3,)), dma((3,)),
+            dma, dma((line, 3)), dma((line,)), dma, dma((2, line)), dma((3,)), dma((3,)),
             dma((2,)), dma((2,)),
         ],
         compiler_params=pltpu.CompilerParams(
@@ -807,7 +854,7 @@
             jax.ShapeDtypeStruct((1, row_count), jnp.float32),
             jax.ShapeDtypeStruct((cents, cents), jnp.float32),
         )
-        if groups == 2 and shards % 4 == 0 and shards > 4 and row_count % 64 == 0 and total <= 2048:
+        if groups == 2 and shards == 16 and row_count % 64 == 0 and total <= 2048:
             call = gather_call(shards, row_count, width, cents, out_shape)
         else:
             call = pl.pallas_call(

time: 28.8 us -> 27.5 us (0.955)
  Pallas kernels: 25.9 us -> 24.6 us
    pallas_call x1, Pallas kernels: 25.9 us -> 24.6 us  [step(): call(group_length, pltpu.with_memory_space_constraint(embeddings, pltpu.H...]
where the time goes in v4:
time: 27.5 us; the launch traced here: 27.4 us
  Pallas kernels  24.6 us (89%)
  between operations  1.29 us (5%)
  other arithmetic  0.87 us (3%)
  local copies, waits for them, and re-layouts  0.61 us (2%)
    pallas_call x1, Pallas kernels, step(): call(group_length, pltpu.with_memory_space_constraint(embeddings, pltpu.H...  24.6 us
    convert_element_type x1, other arithmetic, step(): new_moments = (moment_sums * inverse[:, 0:1]).astype(jnp.bfloat16)  0.87 us

profile of v4, /device:TPU:0, one launch (start us, length us, event | category | flops | bytes accessed | tf_op | source)
XLA Modules:
  0.0 27.4 jit_solution(16662624809364429083)
XLA Ops:
  1.3 24.6 %soft_em.1 = (f32[128,768]{1,0:T(8,128)S(1)}, f32[128,768]{1,0:T(8,128)S(1)}, f32[1,64]{1,0:T(1,128)S(1)}, f32[128,128]{1,0:T(8,128)S(1)}) custom-call(s32[1]{0:T(128)S(6)} %copy.7.length_ref, bf16[64,768]{1,0:T(8,128)(2,1)} %emb_hbm.1, bf16[128,768]{1,0:T(8,128)(2,1)} %cent_hbm.1), custom_call_target="tpu_custom_call" | custom-call | tf_op jit(solution)/shard_map/soft_em/pallas_call | solution.py:885
  25.9 0.1 slice_reduce_fusion
  26.0 0.9 %multiply_convert_fusion = (bf16[128,768]{1,0:T(8,128)(2,1)}, bf16[128,768]{1,0:T(8,128)(2,1)}) fusion(f32[128,768]{1,0:T(8,128)S(1)} %get-tuple-element.9, f32[128]{0:T(128)S(1)} %slice_reduce_fusion, f32[128,768]{1,0:T(8,128)S(1)} %get-tuple-element.7), kind=kLoop, calls=%fused_computation | loop fusion | flops 393216 | bytes 1180160 | tf_op jit(solution)/shard_map/convert_element_type | solution.py:887
  26.9 0.5 %copy.8 = f32[64]{0:T(128)} copy(f32[64]{0:T(128)S(1)} %bitcast.1) | data formatting | bytes 512

commit v5 on v4

--- a/solution.py
+++ b/solution.py
@@ -624,8 +624,9 @@
         mass = 0.0
         weighted = cent_out[...]
         moments = mom_out[...]
-        for n, q in enumerate(orders):
-            weigh(1, q, line + n)
+        for n, (q, weighed) in enumerate(orders):
+            if not weighed:
+                weigh(1, q, line + n)
             block = resp[:, total + n * chunk:total + (n + 1) * chunk]
             mass = mass + mass_of(block)
             weighted = weighted + times(block, rows_all[there, pl.ds(q * 4, 4)].reshape(chunk, width))
@@ -726,15 +727,39 @@
 
     def score_there(j):
         score(False, places[j])
-        state["ready"].append(places[j])
-
-    def sums_there(_):
-        if not state["moments"] or not state["ready"]:
-            return
+        state["ready"].append((places[j], False))
+
+    def lse_from_there():
         if not state["there"]:
             move_parts(there, shards, 1).wait_recv()
             keep_lse(1, whole_lse(there))
             state["there"] = True
+
+    def weigh_there(j):
+        lse_from_there()
+        q = places[j]
+        c_come(False, q).wait_recv()
+        block = rows_all[there, pl.ds(q * 4, 4)].reshape(chunk, width)
+        inner = lax.dot_general(
+            cents_all[0], block, contract_width, preferred_element_type=jnp.float32
+        )
+        first = total + len(state["ready"]) * chunk
+        for r in range(spread):
+            left = r * lanes
+            logits = factor * (inner[:, left:left + lanes] - half_norm)
+            resp[:, first + left:first + left + lanes] = jnp.exp(
+                logits - lse_ref[1, r, pl.ds(q, 1), :]
+            ).astype(jnp.bfloat16)
+        wide = block.astype(jnp.float32)
+        squares[there, pl.ds(q * 4, 4)] = (wide * wide).astype(jnp.bfloat16).reshape(
+            4, row_count, width
+        )
+        state["ready"].append((q, True))
+
+    def sums_there(_):
+        if not state["moments"] or not state["ready"]:
+            return
+        lse_from_there()
         state["mass"] = state["mass"] + add_there(state["ready"])
         state["ready"] = []
 
@@ -755,7 +780,7 @@
         "W": crossed, "Y": lambda j: y_take(places[j]), "H": lambda j: x_take(places[j], 1),
         "G": lambda j: x_take(places[j], 0), "T": lambda j: turn_take(places[j], 0),
         "D": lambda j: turn_take(places[j], 1), "S": lambda j: score(True, places[j]),
-        "s": score_there, "R": own_sums, "M": own_moments, "r": sums_there, "l": write_lik,
+        "s": score_there, "f": weigh_there, "R": own_sums, "M": own_moments, "r": sums_there, "l": write_lik,
     }
     for step in steps:
         acts[step[0]](int(step[1:] or 0))
@@ -784,8 +809,8 @@
     "N0", "N1", "Y0", "E", "O", "N2", "S0", "G1", "H0", "N3", "G0", "Z1",
     "Z0", "F", "I", "T0", "Z2", "W0", "H1", "Z3", "Y1", "C", "A0", "A1",
     "A2", "Y2", "L", "H2", "Y3", "G2", "D0", "H3", "W1", "S1", "D1", "s0",
-    "T1", "S3", "G3", "S2", "s1", "R", "T2", "D2", "M", "T3", "D3", "r",
-    "s2", "l", "s3", "r",
+    "T1", "S3", "G3", "S2", "s1", "T2", "D2", "R", "T3", "M", "D3", "r",
+    "f2", "l", "f3", "r",
 )
 
 

time: 27.5 us -> 27.3 us (level)
  no operation moved by 1% of the time
where the time goes in v5:
time: 27.3 us; the launch traced here: 27.2 us
  Pallas kernels  24.4 us (89%)
  between operations  1.29 us (5%)
  other arithmetic  0.87 us (3%)
  local copies, waits for them, and re-layouts  0.61 us (2%)
    pallas_call x1, Pallas kernels, step(): call(group_length, pltpu.with_memory_space_constraint(embeddings, pltpu.H...  24.4 us
    convert_element_type x1, other arithmetic, step(): new_moments = (moment_sums * inverse[:, 0:1]).astype(jnp.bfloat16)  0.87 us

profile of v5, /device:TPU:0, one launch (start us, length us, event | category | flops | bytes accessed | tf_op | source)
XLA Modules:
  0.0 27.2 jit_solution(9127874955891831836)
XLA Ops:
  1.3 24.4 %soft_em.1 = (f32[128,768]{1,0:T(8,128)S(1)}, f32[128,768]{1,0:T(8,128)S(1)}, f32[1,64]{1,0:T(1,128)S(1)}, f32[128,128]{1,0:T(8,128)S(1)}) custom-call(s32[1]{0:T(128)S(6)} %copy.7.length_ref, bf16[64,768]{1,0:T(8,128)(2,1)} %emb_hbm.1, bf16[128,768]{1,0:T(8,128)(2,1)} %cent_hbm.1), custom_call_target="tpu_custom_call" | custom-call | tf_op jit(solution)/shard_map/soft_em/pallas_call | solution.py:910
  25.7 0.1 slice_reduce_fusion
  25.8 0.9 %multiply_convert_fusion = (bf16[128,768]{1,0:T(8,128)(2,1)}, bf16[128,768]{1,0:T(8,128)(2,1)}) fusion(f32[128,768]{1,0:T(8,128)S(1)} %get-tuple-element.9, f32[128]{0:T(128)S(1)} %slice_reduce_fusion, f32[128,768]{1,0:T(8,128)S(1)} %get-tuple-element.7), kind=kLoop, calls=%fused_computation | loop fusion | flops 393216 | bytes 1180160 | tf_op jit(solution)/shard_map/convert_element_type | solution.py:912
  26.7 0.5 %copy.8 = f32[64]{0:T(128)} copy(f32[64]{0:T(128)S(1)} %bitcast.1) | data formatting | bytes 512

commit v6 on v5

--- a/solution.py
+++ b/solution.py
@@ -808,7 +808,7 @@
 schedule = (
     "N0", "N1", "Y0", "E", "O", "N2", "S0", "G1", "H0", "N3", "G0", "Z1",
     "Z0", "F", "I", "T0", "Z2", "W0", "H1", "Z3", "Y1", "C", "A0", "A1",
-    "A2", "Y2", "L", "H2", "Y3", "G2", "D0", "H3", "W1", "S1", "D1", "s0",
+    "A2", "L", "Y2", "H2", "Y3", "G2", "D0", "H3", "W1", "S1", "D1", "s0",
     "T1", "S3", "G3", "S2", "s1", "T2", "D2", "R", "T3", "M", "D3", "r",
     "f2", "l", "f3", "r",
 )

time: 27.3 us -> 27.2 us (level)
  no operation moved by 1% of the time
where the time goes in v6:
time: 27.2 us; the launch traced here: 27.1 us
  Pallas kernels  24.3 us (89%)
  between operations  1.29 us (5%)
  other arithmetic  0.87 us (3%)
  local copies, waits for them, and re-layouts  0.61 us (2%)
    pallas_call x1, Pallas kernels, step(): call(group_length, pltpu.with_memory_space_constraint(embeddings, pltpu.H...  24.3 us
    convert_element_type x1, other arithmetic, step(): new_moments = (moment_sums * inverse[:, 0:1]).astype(jnp.bfloat16)  0.87 us

profile of v6, /device:TPU:0, one launch (start us, length us, event | category | flops | bytes accessed | tf_op | source)
XLA Modules:
  0.0 27.1 jit_solution(2238367810624924712)
XLA Ops:
  1.3 24.3 %soft_em.1 = (f32[128,768]{1,0:T(8,128)S(1)}, f32[128,768]{1,0:T(8,128)S(1)}, f32[1,64]{1,0:T(1,128)S(1)}, f32[128,128]{1,0:T(8,128)S(1)}) custom-call(s32[1]{0:T(128)S(6)} %copy.7.length_ref, bf16[64,768]{1,0:T(8,128)(2,1)} %emb_hbm.1, bf16[128,768]{1,0:T(8,128)(2,1)} %cent_hbm.1), custom_call_target="tpu_custom_call" | custom-call | tf_op jit(solution)/shard_map/soft_em/pallas_call | solution.py:910
  25.6 0.1 slice_reduce_fusion
  25.7 0.9 %multiply_convert_fusion = (bf16[128,768]{1,0:T(8,128)(2,1)}, bf16[128,768]{1,0:T(8,128)(2,1)}) fusion(f32[128,768]{1,0:T(8,128)S(1)} %get-tuple-element.9, f32[128]{0:T(128)S(1)} %slice_reduce_fusion, f32[128,768]{1,0:T(8,128)S(1)} %get-tuple-element.7), kind=kLoop, calls=%fused_computation | loop fusion | flops 393216 | bytes 1180160 | tf_op jit(solution)/shard_map/convert_element_type | solution.py:912
  26.6 0.5 %copy.8 = f32[64]{0:T(128)} copy(f32[64]{0:T(128)S(1)} %bitcast.1) | data formatting | bytes 512
